TPU v7x, 32 devices: a whole 2x2x4 slice. The times are simulated.
32 devices in a mesh: ctx: 8 (over z, y), head: 4 (over x, core).
Axes of the slice: x: 2, y: 2, z: 4, core: 2. Of those that a mesh axis runs over, the one named last changes fastest.
Arguments:
- queries: bfloat16 [4096, 32, 128], P(('ctx', 'head')), may hold values from -6 to 6
- key_states: bfloat16 [4096, 4, 128], P(('ctx', 'head')), may hold values from -6 to 6
- value_states: bfloat16 [4096, 4, 128], P(('ctx', 'head')), may hold values from -6 to 6
- out_grad: bfloat16 [4096, 32, 128], P(('ctx', 'head')), may hold values from -6 to 6
- log_sums: float32 [32, 4096], P('head', 'ctx'), may hold values from 3 to 6
- row_deltas: float32 [32, 4096], P('head', 'ctx'), may hold values from -10 to 10
- block_pairs: int32 [64, 4], replicated, may hold values from 0 to 63, as said below
- pair_kinds: int32 [64, 4], replicated, may hold values from 0 to 2, as said below
Outputs:
- query_grad: bfloat16 [4096, 32, 128], P(('ctx', 'head'))
- key_grad: bfloat16 [4096, 4, 128], P(('ctx', 'head'))
- value_grad: bfloat16 [4096, 4, 128], P(('ctx', 'head'))
Inputs may be any that keep to these rules, and one draw needn't show every extreme that they name: `block_pairs`: row g lists the key blocks of query block g. Slot 0 names g itself, slot 1 names g - 1, slot 2 names key block 0; slots 3 and up name blocks of shards at least two shards before the shard of g, never of shard 0. The blocks of the live slots of a row are distinct and none is later than g; a slot of kind 0 names block 0. Counting shards of 8 consecutive query blocks, the query blocks of one shard name at most one key block held by any other single shard, and this is reached. `pair_kinds`: 1 marks a full block pair, 2 the pair of a block with itself, 0 an unused slot. Slot 0 is always 2 and no other slot is 2; slot 1 is 0 only for g = 0; slot 2 is 0 exactly for g < 2 and for the query blocks of the second shard.
All inputs are finite; a program needn't handle non-finite values.
Results may differ from a plain program's by a relative error of at most 0.0012.
The roundings to bfloat16 on the way count: a program that leaves them out, or rounds other values in their place, can miss the bound.
Values may be sent and summed in bfloat16 or wider, within the bound.
A program may use at most 64 MiB of HBM per device.

v0:
```python
from functools import partial

import jax
import jax.numpy as jnp
from jax import lax
from jax.experimental import pallas as pl
from jax.experimental.pallas import tpu as pltpu
from jax.sharding import PartitionSpec as P

BLOCK = 64
MESH = pl.DeviceIdType.MESH


def kernel(
    n_ctx,
    n_head,
    n_slot,
    pair_tab,
    kind_tab,
    q_hbm,
    g_hbm,
    k_ref,
    v_ref,
    log_ref,
    delta_ref,
    dq_out,
    dk_out,
    dv_land,
    wide,
    kv_in,
    q_buf,
    g_buf,
    kv_loc,
    outgoing,
    arrived,
    kcat,
    log_rows,
    delta_rows,
    acc,
    acc_hub,
    far_terms,
    dq_buf,
    part,
    ret,
    fin,
    dk_land,
    kv_send,
    kv_recv,
    q_send,
    q_recv,
    g_send,
    g_recv,
    arr_send,
    arr_recv,
    dq_send,
    dq_recv,
    ret_send,
    ret_recv,
    fin_send,
    fin_recv,
):
    rank = lax.axis_index("ctx")
    me = lax.axis_index("head")
    rows = q_hbm.shape[0]
    heads = q_hbm.shape[1] // n_head
    width = q_hbm.shape[2]
    per_src = rows // BLOCK
    blocks = per_src * n_head
    lanes = BLOCK * heads
    keys = n_slot * BLOCK
    scale = width ** (-0.5)

    def peer(d):
        return lax.rem(me // 2 + d // 2, n_head // 2) * 2 + lax.rem(
            lax.rem(me, 2) + lax.rem(d, 2), 2
        )

    barrier = pltpu.get_barrier_semaphore()
    for d in range(1, n_head):
        pl.semaphore_signal(barrier, inc=1, device_id=(rank, peer(d)), device_id_type=MESH)

    def greet(k, c):
        pl.semaphore_signal(
            barrier, inc=1, device_id=(lax.rem(rank + k, n_ctx), me), device_id_type=MESH
        )
        return c

    lax.fori_loop(1, n_ctx, greet, 0)
    for at, source in ((0, k_ref), (width, v_ref)):
        wide[...] = source[...].astype(jnp.float32)
        for h in range(n_head):
            head_rows = wide[pl.ds(h, rows, stride=n_head), :]
            kv_in[h, :, :, at : at + width] = head_rows.reshape(per_src, BLOCK, width).astype(
                jnp.bfloat16
            )
    pl.semaphore_wait(barrier, n_ctx + n_head - 2)

    def kv_copy(p):
        return pltpu.make_async_remote_copy(
            src_ref=kv_in.at[p],
            dst_ref=kv_loc.at[pl.ds(me * per_src, per_src)],
            send_sem=kv_send.at[p],
            recv_sem=kv_recv.at[me],
            device_id=(rank, p),
            device_id_type=MESH,
        )

    def token_copy(src, dst, send, recv, p, j):
        return pltpu.make_async_remote_copy(
            src_ref=src.at[pl.ds(j * BLOCK, BLOCK), pl.ds(pl.multiple_of(p * heads, heads), heads)],
            dst_ref=dst.at[me, j],
            send_sem=send.at[p, j],
            recv_sem=recv.at[me, j],
            device_id=(rank, p),
            device_id_type=MESH,
        )

    def own_copy(src, dst, recv, j):
        return pltpu.make_async_copy(
            src.at[pl.ds(j * BLOCK, BLOCK), pl.ds(pl.multiple_of(me * heads, heads), heads)],
            dst.at[me, j],
            recv.at[me, j],
        )

    far_first = list(range(2, n_head)) + [1]
    for d in far_first:
        kv_copy(peer(d)).start()
    own_kv = pltpu.make_async_copy(
        kv_in.at[me], kv_loc.at[pl.ds(me * per_src, per_src)], kv_recv.at[me]
    )
    own_kv.start()
    for j in range(per_src):
        own_copy(q_hbm, q_buf, q_recv, j).start()
        own_copy(g_hbm, g_buf, g_recv, j).start()
    for j in range(per_src):
        for d in far_first:
            token_copy(q_hbm, q_buf, q_send, q_recv, peer(d), j).start()
            token_copy(g_hbm, g_buf, g_send, g_recv, peer(d), j).start()

    own_kv.wait()
    for d in range(1, n_head):
        p = peer(d)
        kv_here = kv_loc.at[pl.ds(p * per_src, per_src)]
        pltpu.make_async_copy(kv_here, kv_here, kv_recv.at[p]).wait()

    first = rank * blocks

    def wanted_by(s):
        best = jnp.where(rank + 1 == s, blocks - 1, 0)
        for i in range(blocks):
            at = s * blocks + i
            for j in range(3, n_slot):
                local = pair_tab[j, at] - first
                named = (kind_tab[j, at] > 0) & (local >= 0) & (local < blocks)
                best = jnp.where(named, jnp.maximum(best, local), best)
        return best

    def arr_copy(s):
        return pltpu.make_async_remote_copy(
            src_ref=outgoing.at[s],
            dst_ref=arrived.at[rank],
            send_sem=arr_send.at[s],
            recv_sem=arr_recv.at[rank],
            device_id=(s, me),
            device_id_type=MESH,
        )

    def send_block(s, c):
        outgoing[s] = kv_loc[wanted_by(s)]
        arr_copy(s).start()
        return c

    lax.fori_loop(rank + 1, n_ctx, send_block, 0)
    arrived[rank] = kv_loc[0]

    spread = (
        lax.broadcasted_iota(jnp.int32, (BLOCK, lanes), 1) // heads
        == lax.broadcasted_iota(jnp.int32, (BLOCK, lanes), 0)
    ).astype(jnp.float32)
    own_row = lax.broadcasted_iota(jnp.int32, (heads, lanes), 1) % heads == lax.broadcasted_iota(
        jnp.int32, (heads, lanes), 0
    )
    for stat_ref, stat_rows in ((log_ref, log_rows), (delta_ref, delta_rows)):
        for i in range(blocks):
            by_lane = jnp.dot(
                stat_ref[:, i * BLOCK : (i + 1) * BLOCK],
                spread,
                precision=lax.Precision.HIGHEST,
                preferred_element_type=jnp.float32,
            )
            stat_rows[i] = jnp.sum(jnp.where(own_row, by_lane, 0.0), axis=0, keepdims=True)
    acc[...] = jnp.zeros_like(acc)
    acc_hub[...] = jnp.zeros_like(acc_hub)

    def take_block(o, c):
        pltpu.make_async_copy(arrived.at[o], arrived.at[o], arr_recv.at[o]).wait()
        return c

    lax.fori_loop(0, rank, take_block, 0)

    key_row = lax.broadcasted_iota(jnp.int32, (keys, lanes), 0)
    causal = (key_row >= BLOCK) | (
        key_row <= lax.broadcasted_iota(jnp.int32, (keys, lanes), 1) // heads
    )

    def dq_copy(p, j):
        return pltpu.make_async_remote_copy(
            src_ref=dq_buf.at[p, j],
            dst_ref=dq_out.at[
                pl.ds(j * BLOCK, BLOCK), pl.ds(pl.multiple_of(me * heads, heads), heads)
            ],
            send_sem=dq_send.at[p, j],
            recv_sem=dq_recv.at[me, j],
            device_id=(rank, p),
            device_id_type=MESH,
        )

    def own_dq(j):
        return pltpu.make_async_copy(
            dq_buf.at[me, j],
            dq_out.at[pl.ds(j * BLOCK, BLOCK), pl.ds(pl.multiple_of(me * heads, heads), heads)],
            dq_recv.at[me, j],
        )

    def far_owner(i, j):
        at = first + i
        return jnp.where(kind_tab[j, at] > 0, lax.div(pair_tab[j, at], blocks), rank)

    def block_step(t, c):
        d = t // (2 * per_src) * 2 + lax.rem(t, 2)
        j = lax.rem(t // 2, per_src)
        p = peer(d)
        i = p * per_src + j
        pltpu.make_async_copy(q_buf.at[p, j], q_buf.at[p, j], q_recv.at[p, j]).wait()
        pltpu.make_async_copy(g_buf.at[p, j], g_buf.at[p, j], g_recv.at[p, j]).wait()
        kcat[0:BLOCK] = kv_loc[i]
        kcat[BLOCK : 2 * BLOCK] = jnp.where(
            i == 0,
            arrived[jnp.maximum(rank - 1, 0)],
            kv_loc[jnp.maximum(i - 1, 0)],
        )
        kcat[2 * BLOCK : 3 * BLOCK] = arrived[0]
        for slot in range(3, n_slot):
            kcat[slot * BLOCK : (slot + 1) * BLOCK] = arrived[far_owner(i, slot)]
        key_tile = kcat[:, :width]
        value_tile = kcat[:, width:]
        q = q_buf[p, j].astype(jnp.float32).reshape(lanes, width).astype(jnp.bfloat16)
        g = g_buf[p, j].astype(jnp.float32).reshape(lanes, width).astype(jnp.bfloat16)
        nt = (((1,), (1,)), ((), ()))
        scores = lax.dot_general(key_tile, q, nt, preferred_element_type=jnp.float32) * scale
        weights = jnp.exp(scores - log_rows[i])
        slot_mask = jnp.ones((keys, 1), jnp.int32)
        slot_row = lax.broadcasted_iota(jnp.int32, (keys, 1), 0) // BLOCK
        for slot in range(1, n_slot):
            kind = kind_tab[slot, first + i]
            slot_mask = jnp.where(slot_row == slot, kind, slot_mask)
        weights = jnp.where(causal & (slot_mask > 0), weights, 0.0)
        rounded = weights.astype(jnp.bfloat16)
        prob_grad = lax.dot_general(value_tile, g, nt, preferred_element_type=jnp.float32)
        dscore = (weights * (prob_grad - delta_rows[i])).astype(jnp.bfloat16)
        dv = jnp.dot(rounded, g, preferred_element_type=jnp.float32)
        dk = jnp.dot(dscore, q, preferred_element_type=jnp.float32)
        dq = lax.dot_general(
            dscore, key_tile, (((0,), (0,)), ((), ())), preferred_element_type=jnp.float32
        )
        dq_buf[p, j] = (dq * scale).reshape(BLOCK, heads, width).astype(jnp.bfloat16)

        @pl.when(d == 0)
        def _():
            own_dq(j).start()

        @pl.when(d > 0)
        def _():
            dq_copy(p, j).start()

        for u, terms in enumerate((dk, dv)):
            acc[u, i + 1] += terms[:BLOCK]
            acc[u, i] += terms[BLOCK : 2 * BLOCK]
            acc_hub[u] += terms[2 * BLOCK : 3 * BLOCK]
            for slot in range(3, n_slot):
                far_terms[u, i, slot - 3] = terms[slot * BLOCK : (slot + 1) * BLOCK]
        return c

    lax.fori_loop(0, blocks, block_step, 0)

    def ret_copy(u, o):
        return pltpu.make_async_remote_copy(
            src_ref=part.at[u, o],
            dst_ref=ret.at[u, rank],
            send_sem=ret_send.at[u, o],
            recv_sem=ret_recv.at[u, rank],
            device_id=(o, me),
            device_id_type=MESH,
        )

    def send_part(u, o):
        terms = jnp.where(o == 0, acc_hub[u], 0.0) + jnp.where(o == rank - 1, acc[u, 0], 0.0)
        for i in range(blocks):
            for slot in range(3, n_slot):
                terms += jnp.where(far_owner(i, slot) == o, far_terms[u, i, slot - 3], 0.0)
        part[u, o] = terms
        ret_copy(u, o).start()

    def take_part(u, s):
        pltpu.make_async_copy(ret.at[u, s], ret.at[u, s], ret_recv.at[u, s]).wait()
        b = wanted_by(s)
        for i in range(blocks):
            acc[u, i + 1] += jnp.where(b == i, ret[u, s], 0.0)

    def fin_copy(u, p):
        return pltpu.make_async_remote_copy(
            src_ref=fin.at[u, p],
            dst_ref=(dk_land, dv_land)[u].at[me],
            send_sem=fin_send.at[u, p],
            recv_sem=fin_recv.at[u, me],
            device_id=(rank, p),
            device_id_type=MESH,
        )

    def own_fin(u):
        return pltpu.make_async_copy(
            fin.at[u, me], (dk_land, dv_land)[u].at[me], fin_recv.at[u, me]
        )

    def each(step, u):
        def body(k, c):
            step(u, k)
            return c

        return body

    for u in range(2):
        lax.fori_loop(0, rank, each(send_part, u), 0)
    for u in range(2):
        acc[u, 1] += jnp.where(rank == 0, acc_hub[u], 0.0)
        lax.fori_loop(rank + 1, n_ctx, each(take_part, u), 0)
        for i in range(blocks):
            fin[u, i // per_src, i % per_src] = (
                acc[u, i + 1] * scale if u == 0 else acc[u, i + 1]
            ).astype(jnp.bfloat16)
        for d in far_first:
            fin_copy(u, peer(d)).start()
        own_fin(u).start()

    def take_fin(u, land):
        own_fin(u).wait()
        for d in range(1, n_head):
            p = peer(d)
            pltpu.make_async_copy(land.at[p], land.at[p], fin_recv.at[u, p]).wait()

    take_fin(0, dk_land)
    dk_out[...] = by_token(dk_land, wide)

    def sent_block(s, c):
        arr_copy(s).wait_send()
        return c

    lax.fori_loop(rank + 1, n_ctx, sent_block, 0)

    def sent_part(o, c):
        ret_copy(0, o).wait_send()
        ret_copy(1, o).wait_send()
        return c

    lax.fori_loop(0, rank, sent_part, 0)
    for d in range(1, n_head):
        p = peer(d)
        kv_copy(p).wait_send()
        for j in range(per_src):
            token_copy(q_hbm, q_buf, q_send, q_recv, p, j).wait_send()
            token_copy(g_hbm, g_buf, g_send, g_recv, p, j).wait_send()
            dq_copy(p, j).wait_send()
            dq_here = dq_out.at[
                pl.ds(j * BLOCK, BLOCK), pl.ds(pl.multiple_of(p * heads, heads), heads)
            ]
            pltpu.make_async_copy(dq_here, dq_here, dq_recv.at[p, j]).wait()
        for u in range(2):
            fin_copy(u, p).wait_send()
    for j in range(per_src):
        own_dq(j).wait()
    take_fin(1, dv_land)


def by_token(land, wide):
    n_head, per_src, block, width = land.shape
    rows = per_src * block
    for h in range(n_head):
        wide[pl.ds(h, rows, stride=n_head), :] = (
            land[h].astype(jnp.float32).reshape(rows, width)
        )
    return wide[...].astype(land.dtype)


def tail(
    dq_in, dk_in, dv_in, dq_out, dk_out, dv_out, dq_held, dk_held, dv_land, dv_held, wide, loads, stores
):
    pieces = loads.shape[0] - 2
    step = dq_held.shape[0] // pieces
    parts = [pl.ds(k * step, step) for k in range(pieces)]
    load_dv = pltpu.make_async_copy(dv_in, dv_land, loads.at[pieces + 1])
    store_dv = pltpu.make_async_copy(dv_held, dv_out, stores.at[pieces + 1])
    routes = [(dq_in.at[at], dq_held.at[at], dq_out.at[at]) for at in parts]
    routes.append((dk_in, dk_held, dk_out))
    load_dv.start()
    for k, (source, held, _) in enumerate(routes):
        pltpu.make_async_copy(source, held, loads.at[k]).start()
    load_dv.wait()
    dv_held[...] = by_token(dv_land, wide)
    store_dv.start()
    for k, (source, held, target) in enumerate(routes):
        pltpu.make_async_copy(source, held, loads.at[k]).wait()
        pltpu.make_async_copy(held, target, stores.at[k]).start()
    for k, (_, held, target) in enumerate(routes):
        pltpu.make_async_copy(held, target, stores.at[k]).wait()
    store_dv.wait()


def shards(
    n_ctx,
    n_head,
    queries,
    key_states,
    value_states,
    out_grad,
    log_sums,
    row_deltas,
    block_pairs,
    pair_kinds,
):
    rows, all_heads, width = queries.shape
    heads = all_heads // n_head
    n_slot = block_pairs.shape[1]
    per_src = rows // BLOCK
    blocks = per_src * n_head
    lanes = BLOCK * heads
    bf16, f32 = jnp.bfloat16, jnp.float32
    half = (n_head, per_src, BLOCK, width)
    flat = (rows * n_head, width)
    vmem = pl.BlockSpec(memory_space=pltpu.VMEM)
    anywhere = pl.BlockSpec(memory_space=pl.ANY)
    dma = pltpu.SemaphoreType.DMA
    dq, dk, dv = pl.pallas_call(
        partial(kernel, n_ctx, n_head, n_slot),
        out_shape=(
            jax.ShapeDtypeStruct(queries.shape, bf16),
            jax.ShapeDtypeStruct(flat, bf16),
            jax.ShapeDtypeStruct(half, bf16),
        ),
        in_specs=[
            pl.BlockSpec(memory_space=pltpu.SMEM),
            pl.BlockSpec(memory_space=pltpu.SMEM),
            anywhere,
            anywhere,
            vmem,
            vmem,
            vmem,
            vmem,
        ],
        out_specs=(anywhere, vmem, vmem),
        scratch_shapes=[
            pltpu.VMEM(flat, f32),
            pltpu.VMEM((n_head, per_src, BLOCK, 2 * width), bf16),
            pltpu.VMEM((n_head, per_src, BLOCK, heads, width), bf16),
            pltpu.VMEM((n_head, per_src, BLOCK, heads, width), bf16),
            pltpu.VMEM((blocks, BLOCK, 2 * width), bf16),
            pltpu.VMEM((n_ctx, BLOCK, 2 * width), bf16),
            pltpu.VMEM((n_ctx, BLOCK, 2 * width), bf16),
            pltpu.VMEM((n_slot * BLOCK, 2 * width), bf16),
            pltpu.VMEM((blocks, 1, lanes), f32),
            pltpu.VMEM((blocks, 1, lanes), f32),
            pltpu.VMEM((2, blocks + 1, BLOCK, width), f32),
            pltpu.VMEM((2, BLOCK, width), f32),
            pltpu.VMEM((2, blocks, n_slot - 3, BLOCK, width), f32),
            pltpu.VMEM((n_head, per_src, BLOCK, heads, width), bf16),
            pltpu.VMEM((2, n_ctx, BLOCK, width), f32),
            pltpu.VMEM((2, n_ctx, BLOCK, width), f32),
            pltpu.VMEM((2,) + half, bf16),
            pltpu.VMEM(half, bf16),
            dma((n_head,)),
            dma((n_head,)),
            dma((n_head, per_src)),
            dma((n_head, per_src)),
            dma((n_head, per_src)),
            dma((n_head, per_src)),
            dma((n_ctx,)),
            dma((n_ctx,)),
            dma((n_head, per_src)),
            dma((n_head, per_src)),
            dma((2, n_ctx)),
            dma((2, n_ctx)),
            dma((2, n_head)),
            dma((2, n_head)),
        ],
        compiler_params=pltpu.CompilerParams(
            collective_id=0, has_side_effects=True, vmem_limit_bytes=60 * 1024 * 1024
        ),
    )(
        block_pairs.T,
        pair_kinds.T,
        queries,
        out_grad,
        key_states.reshape(flat),
        value_states.reshape(flat),
        log_sums,
        row_deltas,
    )
    dq, dk, dv = pl.pallas_call(
        tail,
        out_shape=(
            jax.ShapeDtypeStruct(queries.shape, bf16),
            jax.ShapeDtypeStruct(flat, bf16),
            jax.ShapeDtypeStruct(flat, bf16),
        ),
        in_specs=[anywhere] * 3,
        out_specs=(anywhere,) * 3,
        scratch_shapes=[
            pltpu.VMEM(queries.shape, bf16),
            pltpu.VMEM(flat, bf16),
            pltpu.VMEM(half, bf16),
            pltpu.VMEM(flat, bf16),
            pltpu.VMEM(flat, f32),
            dma((6,)),
            dma((6,)),
        ],
    )(dq, dk, dv)
    return dq, dk.reshape(key_states.shape), dv.reshape(value_states.shape)


def solution(mesh):
    tokens = P(("ctx", "head"), None, None)
    stats = P("head", "ctx")
    return jax.shard_map(
        partial(shards, mesh.shape["ctx"], mesh.shape["head"]),
        mesh=mesh,
        in_specs=(tokens, tokens, tokens, tokens, stats, stats, P(), P()),
        out_specs=(tokens, tokens, tokens),
        check_vma=False,
    )
```

profile of v0, /device:TPU:0, one launch (start us, length us, event | category | flops | bytes accessed | tf_op | source)
XLA Modules:
  0.0 53.5 jit_solution(11325774480827360199)
XLA Ops:
  0.6 50.7 %shard_map.103 = (bf16[128,32,128]{2,1,0:T(8,128)(2,1)}, bf16[512,128]{1,0:T(8,128)(2,1)}, bf16[4,2,64,128]{3,2,1,0:T(8,128)(2,1)}) custom-call(s32[4,64]{1,0:T(4,128)} %bitcast.8, s32[4,64]{1,0:T(4,128)} %bitcast.9, bf16[128,32,128]{2,1,0:T(8,128)(2,1)} %q_hbm.1, bf16[128,32,128]{2,1,0:T(8,128)(2,1)} %g_hbm.1, bf16[512,128]{1,0:T(8,128)(2,1)} %bitcast.6, ...), custom_call_target="tpu_custom_call" | custom-call | tf_op jit(solution)/shard_map/pallas_call | solution.py:442
  51.3 2.1 %shard_map.104 = (bf16[128,32,128]{2,1,0:T(8,128)(2,1)}, bf16[512,128]{1,0:T(8,128)(2,1)}, bf16[512,128]{1,0:T(8,128)(2,1)}) custom-call(bf16[128,32,128]{2,1,0:T(8,128)(2,1)} %get-tuple-element.9.dq_in, bf16[512,128]{1,0:T(8,128)(2,1)} %get-tuple-element.10.dk_in, bf16[4,2,64,128]{3,2,1,0:T(8,128)(2,1)} %get-tuple-element.11.dv_in), custom_call_target="tpu_custom_call" | custom-call | tf_op jit(solution)/shard_map/pallas_call | solution.py:507
where the time goes:
time: 53.6 us; the launch traced here: 53.5 us
  Pallas kernels  52.8 us (99%)
  between operations  0.64 us (1%)
    pallas_call x1, Pallas kernels, shards(): pl.pallas_call(partial(kernel, n_ctx, n_head, n_slot), out_shape=(jax.Sha...  50.7 us
    pallas_call x1, Pallas kernels, shards(): pl.pallas_call(tail, out_shape=(jax.ShapeDtypeStruct(queries.shape, bf16)...  2.13 us

commit v1 on v0

v1 whole, which is shorter than its diff:
```python
from functools import partial

import jax
import jax.numpy as jnp
from jax import lax
from jax.experimental import pallas as pl
from jax.experimental.pallas import tpu as pltpu
from jax.sharding import PartitionSpec as P

BLOCK = 64
NEAR = 3
MESH = pl.DeviceIdType.MESH
NT = (((1,), (1,)), ((), ()))
TN = (((0,), (0,)), ((), ()))


def tile_grads(keys, values, q, g, log_row, delta_row, live, scale):
    scores = lax.dot_general(keys, q, NT, preferred_element_type=jnp.float32) * scale
    weights = jnp.where(live, jnp.exp(scores - log_row), 0.0)
    prob_grad = lax.dot_general(values, g, NT, preferred_element_type=jnp.float32)
    dscore = (weights * (prob_grad - delta_row)).astype(jnp.bfloat16)
    dv = jnp.dot(weights.astype(jnp.bfloat16), g, preferred_element_type=jnp.float32)
    dk = jnp.dot(dscore, q, preferred_element_type=jnp.float32)
    dq = lax.dot_general(dscore, keys, TN, preferred_element_type=jnp.float32)
    return dq, dk, dv


def kernel(
    n_ctx,
    n_head,
    n_slot,
    pair_tab,
    kind_tab,
    q_hbm,
    g_hbm,
    k_ref,
    v_ref,
    log_ref,
    delta_ref,
    dq_out,
    dk_out,
    dv_out,
    wide,
    kv_own,
    kv_loc,
    kv_prev,
    outgoing,
    arrived,
    late_send,
    late_kv,
    q_raw,
    g_raw,
    q_flat,
    g_flat,
    stat_land,
    stat_rows,
    dq_acc,
    dq_buf,
    own_acc,
    prev_part,
    prev_land,
    late_part,
    late_land,
    part,
    ret,
    blk_part,
    blk_land,
    want,
    owner,
    load_sem,
    kv_send,
    kv_recv,
    stat_send,
    stat_recv,
    prev_send,
    prev_recv,
    arr_send,
    arr_recv,
    late_ssem,
    late_rsem,
    dq_sem,
    back_send,
    back_recv,
    red_send,
    red_recv,
    ret_send,
    ret_recv,
    blk_send,
    blk_recv,
):
    rank = lax.axis_index("ctx")
    me = lax.axis_index("head")
    rows = q_hbm.shape[0]
    width = q_hbm.shape[2]
    heads = q_hbm.shape[1] // n_head
    per = rows // BLOCK
    blocks = per * n_head
    lanes = BLOCK * heads
    n_far = n_slot - NEAR
    n_late = 1 + n_far
    scale = width ** (-0.5)
    first = rank * blocks
    bf16, f32 = jnp.bfloat16, jnp.float32

    def peer(d):
        return lax.rem(me // 2 + d // 2, n_head // 2) * 2 + lax.rem(
            lax.rem(me, 2) + lax.rem(d, 2), 2
        )

    far_first = list(range(2, n_head)) + [1]
    has_prev = (rank > 0) | (me > 0)
    has_next = (rank < n_ctx - 1) | (me < n_head - 1)
    prev_dev = (jnp.where(me > 0, rank, rank - 1), jnp.where(me > 0, me - 1, n_head - 1))
    next_dev = (
        jnp.where(me < n_head - 1, rank, rank + 1),
        jnp.where(me < n_head - 1, me + 1, 0),
    )
    outer_prev = (me == 0) & (rank > 0)
    outer_next = (me == n_head - 1) & (rank < n_ctx - 1)
    take_lo = jnp.where(rank == 0, 1, rank + 2)
    owes = (rank == 0) | (rank < n_ctx - 2)

    barrier = pltpu.get_barrier_semaphore()
    for d in range(1, n_head):
        pl.semaphore_signal(barrier, inc=1, device_id=(rank, peer(d)), device_id_type=MESH)

    def greet(k, c):
        pl.semaphore_signal(
            barrier, inc=1, device_id=(lax.rem(rank + k, n_ctx), me), device_id_type=MESH
        )
        return c

    lax.fori_loop(1, n_ctx, greet, 0)

    @pl.when(outer_prev)
    def _():
        pl.semaphore_signal(barrier, inc=1, device_id=prev_dev, device_id_type=MESH)

    @pl.when(outer_next)
    def _():
        pl.semaphore_signal(barrier, inc=1, device_id=next_dev, device_id_type=MESH)

    def load_copy(u, k, j):
        return pltpu.make_async_copy(
            (q_hbm, g_hbm)[u].at[
                pl.ds(j * BLOCK, BLOCK), pl.ds(pl.multiple_of(k * heads, heads), heads)
            ],
            (q_raw, g_raw)[u].at[k, j],
            load_sem.at[u, k, j],
        )

    for u in range(2):
        for k in range(n_head):
            for j in range(per):
                load_copy(u, k, j).start()

    for at, source in ((0, k_ref), (width, v_ref)):
        wide[...] = source[...].astype(f32)
        for h in range(n_head):
            head_rows = wide[pl.ds(h, rows, stride=n_head), :]
            kv_own[h, :, :, at : at + width] = head_rows.reshape(per, BLOCK, width).astype(bf16)

    def wanted_by(s, c):
        best = jnp.int32(0)
        for i in range(blocks):
            at = s * blocks + i
            for j in range(NEAR, n_slot):
                local = pair_tab[j, at] - first
                named = (kind_tab[j, at] > 0) & (local >= 0) & (local < blocks)
                best = jnp.where(named, jnp.maximum(best, local), best)
        want[s] = best
        return c

    lax.fori_loop(take_lo, n_ctx, wanted_by, 0)
    for i in range(blocks):
        for f in range(n_far):
            at = first + i
            owner[i * n_far + f] = jnp.where(
                kind_tab[NEAR + f, at] > 0, lax.div(pair_tab[NEAR + f, at], blocks), rank
            )

    @pl.when(jnp.logical_not(has_prev))
    def _():
        kv_prev[...] = jnp.zeros_like(kv_prev)

    def flatten(t, c):
        k, j = t // per, lax.rem(t, per)
        for u, (raw, flat) in enumerate(((q_raw, q_flat), (g_raw, g_flat))):
            load_copy(u, k, j).wait()
            flat[k, j] = raw[k, j].astype(f32).reshape(lanes, width).astype(bf16)
        return c

    lax.fori_loop(0, n_head * per, flatten, 0)

    extra = outer_prev.astype(jnp.int32) + outer_next.astype(jnp.int32)
    pl.semaphore_wait(barrier, n_ctx + n_head - 2 + extra)

    def kv_copy(p):
        return pltpu.make_async_remote_copy(
            src_ref=kv_own.at[p],
            dst_ref=kv_loc.at[pl.ds(me * per, per)],
            send_sem=kv_send.at[p],
            recv_sem=kv_recv.at[me],
            device_id=(rank, p),
            device_id_type=MESH,
        )

    def stat_copy(u, p):
        return pltpu.make_async_remote_copy(
            src_ref=(log_ref, delta_ref)[u].at[:, pl.ds(pl.multiple_of(p * rows, rows), rows)],
            dst_ref=stat_land.at[u, me],
            send_sem=stat_send.at[u, p],
            recv_sem=stat_recv.at[u, me],
            device_id=(rank, p),
            device_id_type=MESH,
        )

    def prev_copy():
        return pltpu.make_async_remote_copy(
            src_ref=kv_own.at[:, per - 1],
            dst_ref=kv_prev,
            send_sem=prev_send.at[0],
            recv_sem=prev_recv.at[0],
            device_id=next_dev,
            device_id_type=MESH,
        )

    for d in far_first:
        kv_copy(peer(d)).start()
    for u in range(2):
        for d in far_first:
            stat_copy(u, peer(d)).start()

    @pl.when(has_next)
    def _():
        prev_copy().start()

    kv_loc[pl.ds(me * per, per)] = kv_own[me]
    for u, source in enumerate((log_ref, delta_ref)):
        stat_land[u, me] = source[:, pl.ds(pl.multiple_of(me * rows, rows), rows)]

    for d in range(1, n_head):
        p = peer(d)
        kv_here = kv_loc.at[pl.ds(p * per, per)]
        pltpu.make_async_copy(kv_here, kv_here, kv_recv.at[p]).wait()

    def arr_copy(s):
        return pltpu.make_async_remote_copy(
            src_ref=outgoing.at[s],
            dst_ref=arrived.at[rank],
            send_sem=arr_send.at[s],
            recv_sem=arr_recv.at[rank],
            device_id=(s, me),
            device_id_type=MESH,
        )

    def send_block(s, c):
        outgoing[s] = kv_loc[want[s]]
        arr_copy(s).start()
        return c

    lax.fori_loop(take_lo, n_ctx, send_block, 0)
    arrived[rank] = kv_loc[0]

    for d in range(1, n_head):
        p = peer(d)
        for u in range(2):
            here = stat_land.at[u, p]
            pltpu.make_async_copy(here, here, stat_recv.at[u, p]).wait()
    spread = (
        lax.broadcasted_iota(jnp.int32, (BLOCK, lanes), 1) // heads
        == lax.broadcasted_iota(jnp.int32, (BLOCK, lanes), 0)
    ).astype(bf16)
    own_row = lax.broadcasted_iota(jnp.int32, (heads, lanes), 1) % heads == lax.broadcasted_iota(
        jnp.int32, (heads, lanes), 0
    )
    stats = stat_land[...].reshape(2 * n_head * heads, rows)
    high = stats.astype(bf16)
    rest = stats - high.astype(f32)
    mid = rest.astype(bf16)
    low = (rest - mid.astype(f32)).astype(bf16)
    for j in range(per):
        at = slice(j * BLOCK, (j + 1) * BLOCK)
        by_lane = sum(
            jnp.dot(piece[:, at], spread, preferred_element_type=f32) for piece in (high, mid, low)
        ).reshape(2 * n_head, heads, lanes)
        stat_rows[j] = jnp.sum(jnp.where(own_row[None], by_lane, 0.0), axis=1)

    @pl.when(has_prev)
    def _():
        pltpu.make_async_copy(kv_prev, kv_prev, prev_recv.at[0]).wait()

    def back_copy(k):
        return pltpu.make_async_remote_copy(
            src_ref=prev_part.at[k],
            dst_ref=prev_land.at[k],
            send_sem=back_send.at[k],
            recv_sem=back_recv.at[k],
            device_id=prev_dev,
            device_id_type=MESH,
        )

    key_row = lax.broadcasted_iota(jnp.int32, (2 * BLOCK, lanes), 0)
    causal = (key_row >= BLOCK) | (
        key_row <= lax.broadcasted_iota(jnp.int32, (2 * BLOCK, lanes), 1) // heads
    )
    pair_row = lax.broadcasted_iota(jnp.int32, (2 * BLOCK, 1), 0)

    for j in range(per):
        prev_kind = kind_tab[1, first + me * per + j]
        near_live = causal & (jnp.where(pair_row < BLOCK, 1, prev_kind) > 0)

        def near_step(k, c, j=j, near_live=near_live):
            before = kv_prev[k] if j == 0 else kv_own[k, j - 1]
            kv = jnp.concatenate([kv_own[k, j], before], axis=0)
            dq, dk, dv = tile_grads(
                kv[:, :width],
                kv[:, width:],
                q_flat[k, j],
                g_flat[k, j],
                stat_rows[j, pl.ds(k, 1)],
                stat_rows[j, pl.ds(n_head + k, 1)],
                near_live,
                scale,
            )
            dq_acc[k, j] = dq
            for u, terms in enumerate((dk, dv)):
                own_acc[u, k, j] = terms[:BLOCK]
                if j == 0:
                    prev_part[k, u] = terms[BLOCK:]
                else:
                    own_acc[u, k, j - 1] += terms[BLOCK:]
            if j == 0:

                @pl.when(has_prev)
                def _():
                    back_copy(k).start()

            return c

        lax.fori_loop(0, n_head, near_step, 0, unroll=2)

    def arr_wait(o, c):
        pltpu.make_async_copy(arrived.at[o], arrived.at[o], arr_recv.at[o]).wait()
        return c

    @pl.when(rank > 0)
    def _():
        arr_wait(0, 0)

    lax.fori_loop(1, rank - 1, arr_wait, 0)

    def late_copy(p):
        return pltpu.make_async_remote_copy(
            src_ref=late_send.at[p],
            dst_ref=late_kv.at[me],
            send_sem=late_ssem.at[p],
            recv_sem=late_rsem.at[me],
            device_id=(rank, p),
            device_id_type=MESH,
        )

    def fill_late(buf, at, p):
        buf[at, 0] = arrived[0]
        for j in range(per):
            for f in range(n_far):
                buf[at, 1 + j * n_far + f] = arrived[owner[(p * per + j) * n_far + f]]

    for d in far_first:
        p = peer(d)
        fill_late(late_send, p, p)
        late_copy(p).start()
    fill_late(late_kv, me, me)
    for d in range(1, n_head):
        p = peer(d)
        pltpu.make_async_copy(late_kv.at[p], late_kv.at[p], late_rsem.at[p]).wait()

    def red_copy(u, k):
        return pltpu.make_async_remote_copy(
            src_ref=late_part.at[k, u],
            dst_ref=late_land.at[me, u],
            send_sem=red_send.at[u, k],
            recv_sem=red_recv.at[u, me],
            device_id=(rank, k),
            device_id_type=MESH,
        )

    def dq_copy(k, j):
        return pltpu.make_async_copy(
            dq_buf.at[k, j],
            dq_out.at[
                pl.ds(j * BLOCK, BLOCK), pl.ds(pl.multiple_of(k * heads, heads), heads)
            ],
            dq_sem.at[k, j],
        )

    late_row = lax.broadcasted_iota(jnp.int32, (n_late * BLOCK, 1), 0) // BLOCK

    def late_step(k):
        for j in range(per):
            live = jnp.zeros((n_late * BLOCK, 1), jnp.int32)
            for f in range(n_late):
                kind = kind_tab[NEAR - 1 + f, first + me * per + j]
                live = jnp.where(late_row == f, kind, live)
            kv = jnp.concatenate(
                [late_kv[k, 0]] + [late_kv[k, 1 + j * n_far + f] for f in range(n_far)], axis=0
            )
            dq, dk, dv = tile_grads(
                kv[:, :width],
                kv[:, width:],
                q_flat[k, j],
                g_flat[k, j],
                stat_rows[j, pl.ds(k, 1)],
                stat_rows[j, pl.ds(n_head + k, 1)],
                live > 0,
                scale,
            )
            dq_buf[k, j] = ((dq_acc[k, j] + dq) * scale).reshape(BLOCK, heads, width).astype(bf16)
            dq_copy(k, j).start()
            for u, terms in enumerate((dk, dv)):
                if j == 0:
                    late_part[k, u, 0] = terms[:BLOCK]
                else:
                    late_part[k, u, 0] += terms[:BLOCK]
                for f in range(n_far):
                    late_part[k, u, 1 + j * n_far + f] = terms[(1 + f) * BLOCK : (2 + f) * BLOCK]

    def late_remote(t, c):
        k = peer(jnp.where(t < n_head - 2, t + 2, 1))
        late_step(k)
        for u in range(2):
            red_copy(u, k).start()
        return c

    lax.fori_loop(0, n_head - 1, late_remote, 0)
    late_step(me)

    def ret_copy(u, o):
        return pltpu.make_async_remote_copy(
            src_ref=part.at[u, o],
            dst_ref=ret.at[u, rank],
            send_sem=ret_send.at[u, o],
            recv_sem=ret_recv.at[u, rank],
            device_id=(o, me),
            device_id_type=MESH,
        )

    sources = [(peer(d), late_land) for d in range(1, n_head)] + [(me, late_part)]
    for u in range(2):
        for d in range(1, n_head):
            here = late_land.at[peer(d), u]
            pltpu.make_async_copy(here, here, red_recv.at[u, peer(d)]).wait()
        part[u, 0] = sum(buf[p, u, 0] for p, buf in sources)

        @pl.when(rank > 0)
        def _():
            ret_copy(u, 0).start()

        def send_part(o, c):
            terms = jnp.zeros((BLOCK, width), f32)
            for p, buf in sources:
                for j in range(per):
                    for f in range(n_far):
                        mine = owner[(p * per + j) * n_far + f] == o
                        terms += jnp.where(mine, buf[p, u, 1 + j * n_far + f], 0.0)
            part[u, o] = terms
            ret_copy(u, o).start()
            return c

        lax.fori_loop(1, rank - 1, send_part, 0)

    def blk_copy(u, p):
        return pltpu.make_async_remote_copy(
            src_ref=blk_part.at[p, u],
            dst_ref=blk_land.at[me, u],
            send_sem=blk_send.at[u, p],
            recv_sem=blk_recv.at[u, me],
            device_id=(rank, p),
            device_id_type=MESH,
        )

    @pl.when(owes)
    def _():
        for u in range(2):
            blk_part[:, u] = jnp.zeros((n_head, per, BLOCK, width), f32)

            @pl.when(rank == 0)
            def _():
                blk_part[0, u, 0] = part[u, 0]

            def take_part(s, c):
                pltpu.make_async_copy(ret.at[u, s], ret.at[u, s], ret_recv.at[u, s]).wait()
                for i in range(blocks):
                    blk_part[i // per, u, i % per] += jnp.where(want[s] == i, ret[u, s], 0.0)
                return c

            lax.fori_loop(take_lo, n_ctx, take_part, 0)
            for d in far_first:
                blk_copy(u, peer(d)).start()

    @pl.when(has_next)
    def _():
        for k in range(n_head):
            pltpu.make_async_copy(prev_land.at[k], prev_land.at[k], back_recv.at[k]).wait()
            for u in range(2):
                own_acc[u, k, per - 1] += prev_land[k, u]

    @pl.when(owes)
    def _():
        for u in range(2):
            own_acc[u, me] += blk_part[me, u]
            for d in range(1, n_head):
                p = peer(d)
                here = blk_land.at[p, u]
                pltpu.make_async_copy(here, here, blk_recv.at[u, p]).wait()
                own_acc[u, p] += blk_land[p, u]

    for u, out in ((0, dk_out), (1, dv_out)):
        for h in range(n_head):
            terms = own_acc[u, h].reshape(rows, width)
            wide[pl.ds(h, rows, stride=n_head), :] = terms * scale if u == 0 else terms
        out[...] = wide[...].astype(bf16)

    def sent_block(s, c):
        arr_copy(s).wait_send()
        return c

    lax.fori_loop(take_lo, n_ctx, sent_block, 0)

    def sent_part(o, c):
        ret_copy(0, o).wait_send()
        ret_copy(1, o).wait_send()
        return c

    @pl.when(rank > 0)
    def _():
        sent_part(0, 0)

    lax.fori_loop(1, rank - 1, sent_part, 0)
    for d in range(1, n_head):
        p = peer(d)
        kv_copy(p).wait_send()
        late_copy(p).wait_send()
        for u in range(2):
            stat_copy(u, p).wait_send()
            red_copy(u, p).wait_send()

    @pl.when(owes)
    def _():
        for d in range(1, n_head):
            for u in range(2):
                blk_copy(u, peer(d)).wait_send()

    @pl.when(has_next)
    def _():
        prev_copy().wait_send()

    @pl.when(has_prev)
    def _():
        for k in range(n_head):
            back_copy(k).wait_send()

    for k in range(n_head):
        for j in range(per):
            dq_copy(k, j).wait()


def tail(dq_in, dk_in, dv_in, dq_out, dk_out, dv_out, dq_held, dk_held, dv_held, loads, stores):
    pieces = loads.shape[0] - 2
    step = dq_held.shape[0] // pieces
    parts = [pl.ds(k * step, step) for k in range(pieces)]
    routes = [(dq_in.at[at], dq_held.at[at], dq_out.at[at]) for at in parts]
    routes += [(dk_in, dk_held, dk_out), (dv_in, dv_held, dv_out)]
    for k, (source, held, _) in enumerate(routes):
        pltpu.make_async_copy(source, held, loads.at[k]).start()
    for k, (source, held, target) in enumerate(routes):
        pltpu.make_async_copy(source, held, loads.at[k]).wait()
        pltpu.make_async_copy(held, target, stores.at[k]).start()
    for k, (_, held, target) in enumerate(routes):
        pltpu.make_async_copy(held, target, stores.at[k]).wait()


def shards(
    n_ctx,
    n_head,
    queries,
    key_states,
    value_states,
    out_grad,
    log_sums,
    row_deltas,
    block_pairs,
    pair_kinds,
):
    rows, all_heads, width = queries.shape
    heads = all_heads // n_head
    n_slot = block_pairs.shape[1]
    n_far = n_slot - NEAR
    per = rows // BLOCK
    blocks = per * n_head
    lanes = BLOCK * heads
    n_late = 1 + per * n_far
    bf16, f32 = jnp.bfloat16, jnp.float32
    flat = (rows * n_head, width)
    kv = (BLOCK, 2 * width)
    term = (BLOCK, width)
    vmem = pl.BlockSpec(memory_space=pltpu.VMEM)
    smem = pl.BlockSpec(memory_space=pltpu.SMEM)
    anywhere = pl.BlockSpec(memory_space=pl.ANY)
    dma = pltpu.SemaphoreType.DMA
    raw = pltpu.VMEM((n_head, per, BLOCK, heads, width), bf16)
    rolled = pltpu.VMEM((n_head, per, lanes, width), bf16)
    dq, dk, dv = pl.pallas_call(
        partial(kernel, n_ctx, n_head, n_slot),
        out_shape=(
            jax.ShapeDtypeStruct(queries.shape, bf16),
            jax.ShapeDtypeStruct(flat, bf16),
            jax.ShapeDtypeStruct(flat, bf16),
        ),
        in_specs=[smem, smem, anywhere, anywhere, vmem, vmem, vmem, vmem],
        out_specs=(anywhere, vmem, vmem),
        scratch_shapes=[
            pltpu.VMEM(flat, f32),
            pltpu.VMEM((n_head, per) + kv, bf16),
            pltpu.VMEM((blocks,) + kv, bf16),
            pltpu.VMEM((n_head,) + kv, bf16),
            pltpu.VMEM((n_ctx,) + kv, bf16),
            pltpu.VMEM((n_ctx,) + kv, bf16),
            pltpu.VMEM((n_head, n_late) + kv, bf16),
            pltpu.VMEM((n_head, n_late) + kv, bf16),
            raw,
            raw,
            rolled,
            rolled,
            pltpu.VMEM((2, n_head, heads, rows), f32),
            pltpu.VMEM((per, 2 * n_head, lanes), f32),
            pltpu.VMEM((n_head, per, lanes, width), f32),
            raw,
            pltpu.VMEM((2, n_head, per) + term, f32),
            pltpu.VMEM((n_head, 2) + term, f32),
            pltpu.VMEM((n_head, 2) + term, f32),
            pltpu.VMEM((n_head, 2, n_late) + term, f32),
            pltpu.VMEM((n_head, 2, n_late) + term, f32),
            pltpu.VMEM((2, n_ctx) + term, f32),
            pltpu.VMEM((2, n_ctx) + term, f32),
            pltpu.VMEM((n_head, 2, per) + term, f32),
            pltpu.VMEM((n_head, 2, per) + term, f32),
            pltpu.SMEM((n_ctx,), jnp.int32),
            pltpu.SMEM((blocks * n_far,), jnp.int32),
            dma((2, n_head, per)),
            dma((n_head,)),
            dma((n_head,)),
            dma((2, n_head)),
            dma((2, n_head)),
            dma((1,)),
            dma((1,)),
            dma((n_ctx,)),
            dma((n_ctx,)),
            dma((n_head,)),
            dma((n_head,)),
            dma((n_head, per)),
            dma((n_head,)),
            dma((n_head,)),
            dma((2, n_head)),
            dma((2, n_head)),
            dma((2, n_ctx)),
            dma((2, n_ctx)),
            dma((2, n_head)),
            dma((2, n_head)),
        ],
        compiler_params=pltpu.CompilerParams(
            collective_id=0, has_side_effects=True, vmem_limit_bytes=60 * 1024 * 1024
        ),
    )(
        block_pairs.T,
        pair_kinds.T,
        queries,
        out_grad,
        key_states.reshape(flat),
        value_states.reshape(flat),
        log_sums,
        row_deltas,
    )
    dq, dk, dv = pl.pallas_call(
        tail,
        out_shape=(
            jax.ShapeDtypeStruct(queries.shape, bf16),
            jax.ShapeDtypeStruct(flat, bf16),
            jax.ShapeDtypeStruct(flat, bf16),
        ),
        in_specs=[anywhere] * 3,
        out_specs=(anywhere,) * 3,
        scratch_shapes=[
            pltpu.VMEM(queries.shape, bf16),
            pltpu.VMEM(flat, bf16),
            pltpu.VMEM(flat, bf16),
            dma((6,)),
            dma((6,)),
        ],
    )(dq, dk, dv)
    return dq, dk.reshape(key_states.shape), dv.reshape(value_states.shape)


def solution(mesh):
    tokens = P(("ctx", "head"), None, None)
    stats = P("head", "ctx")
    return jax.shard_map(
        partial(shards, mesh.shape["ctx"], mesh.shape["head"]),
        mesh=mesh,
        in_specs=(tokens, tokens, tokens, tokens, stats, stats, P(), P()),
        out_specs=(tokens, tokens, tokens),
        check_vma=False,
    )
```

time: 53.6 us -> 53.8 us (level)
  the two profiles are of different devices: /device:TPU:0 before, /device:TPU:11 now
where the time goes in v1:
time: 53.8 us; the launch traced here: 53.6 us
  Pallas kernels  52.9 us (98%)
  between operations  0.64 us (1%)
    pallas_call x1, Pallas kernels, shards(): pl.pallas_call(partial(kernel, n_ctx, n_head, n_slot), out_shape=(jax.Sha...  50.8 us
    pallas_call x1, Pallas kernels, shards(): pl.pallas_call(tail, out_shape=(jax.ShapeDtypeStruct(queries.shape, bf16)...  2.1 us

profile of v1, /device:TPU:11, one launch (start us, length us, event | category | flops | bytes accessed | tf_op | source)
XLA Modules:
  0.0 53.6 jit_solution(11356038305918564313)
XLA Ops:
  0.6 50.8 %shard_map.103 = (bf16[128,32,128]{2,1,0:T(8,128)(2,1)}, bf16[512,128]{1,0:T(8,128)(2,1)}, bf16[512,128]{1,0:T(8,128)(2,1)}) custom-call(s32[4,64]{1,0:T(4,128)} %bitcast.8, s32[4,64]{1,0:T(4,128)} %bitcast.9, bf16[128,32,128]{2,1,0:T(8,128)(2,1)} %q_hbm.1, bf16[128,32,128]{2,1,0:T(8,128)(2,1)} %g_hbm.1, bf16[512,128]{1,0:T(8,128)(2,1)} %bitcast.6, ...), custom_call_target="tpu_custom_call" | custom-call | tf_op jit(solution)/shard_map/pallas_call | solution.py:613
  51.5 2.1 %shard_map.104 = (bf16[128,32,128]{2,1,0:T(8,128)(2,1)}, bf16[512,128]{1,0:T(8,128)(2,1)}, bf16[512,128]{1,0:T(8,128)(2,1)}) custom-call(bf16[128,32,128]{2,1,0:T(8,128)(2,1)} %get-tuple-element.9.dq_in, bf16[512,128]{1,0:T(8,128)(2,1)} %get-tuple-element.10.dk_in, bf16[512,128]{1,0:T(8,128)(2,1)} %get-tuple-element.11.dv_in), custom_call_target="tpu_custom_call" | custom-call | tf_op jit(solution)/shard_map/pallas_call | solution.py:684

commit v2 on v1

v2 whole, which is shorter than its diff:
```python
from functools import partial

import jax
import jax.numpy as jnp
from jax import lax
from jax.experimental import pallas as pl
from jax.experimental.pallas import tpu as pltpu
from jax.sharding import PartitionSpec as P

BLOCK = 64
NEAR = 3
CUTS = 2
MESH = pl.DeviceIdType.MESH
NT = (((1,), (1,)), ((), ()))
TN = (((0,), (0,)), ((), ()))


def tile_grads(keys, values, q, g, log_row, delta_row, live, scale):
    scores = lax.dot_general(keys, q, NT, preferred_element_type=jnp.float32) * scale
    weights = jnp.where(live, jnp.exp(scores - log_row), 0.0)
    prob_grad = lax.dot_general(values, g, NT, preferred_element_type=jnp.float32)
    dscore = (weights * (prob_grad - delta_row)).astype(jnp.bfloat16)
    dv = jnp.dot(weights.astype(jnp.bfloat16), g, preferred_element_type=jnp.float32)
    dk = jnp.dot(dscore, q, preferred_element_type=jnp.float32)
    dq = lax.dot_general(dscore, keys, TN, preferred_element_type=jnp.float32)
    return dq, dk, dv


def kernel(
    n_ctx,
    n_head,
    n_slot,
    pair_tab,
    kind_tab,
    q_hbm,
    g_hbm,
    k_ref,
    v_ref,
    log_ref,
    delta_ref,
    dq_out,
    dk_out,
    dv_out,
    wide,
    kv_own,
    kv_loc,
    kv_prev,
    outgoing,
    arrived,
    far_send,
    far_kv,
    hub_kv,
    q_raw,
    g_raw,
    q_flat,
    g_flat,
    stat_land,
    stat_rows,
    dq_acc,
    dq_buf,
    own_acc,
    prev_part,
    prev_land,
    far_part,
    far_land,
    hub_part,
    hub_land,
    hub_pair,
    hub_sum,
    hub_tree,
    hub_last,
    part,
    ret,
    blk_part,
    blk_land,
    want,
    owner,
    load_sem,
    kv_sem,
    stat_sem,
    prev_sem,
    arr_send,
    arr_recv,
    far_sem,
    hub_sem,
    dq_sem,
    back_sem,
    hred_sem,
    pair_sem,
    tree_send,
    tree_recv,
    last_sem,
    red_send,
    red_recv,
    ret_send,
    ret_recv,
    blk_send,
    blk_recv,
):
    rank = lax.axis_index("ctx")
    me = lax.axis_index("head")
    rows = q_hbm.shape[0]
    width = q_hbm.shape[2]
    heads = q_hbm.shape[1] // n_head
    per = rows // BLOCK
    blocks = per * n_head
    lanes = BLOCK * heads
    n_far = n_slot - NEAR
    here_far = per * n_far
    stages = tree_recv.shape[0]
    chunks, piece = part.shape[1], part.shape[2]
    cuts = BLOCK // piece
    others = n_head - 1
    scale = width ** (-0.5)
    first = rank * blocks
    bf16, f32 = jnp.bfloat16, jnp.float32

    def peer(d):
        return lax.rem(me // 2 + d // 2, n_head // 2) * 2 + lax.rem(
            lax.rem(me, 2) + lax.rem(d, 2), 2
        )

    def arrive(ref, sem):
        pltpu.make_async_copy(ref, ref, sem).wait()

    def remote(source, target, send, recv, device):
        return pltpu.make_async_remote_copy(
            src_ref=source,
            dst_ref=target,
            send_sem=send,
            recv_sem=recv,
            device_id=device,
            device_id_type=MESH,
        )

    far_first = list(range(2, n_head)) + [1]
    across = far_first[:-1]
    has_prev = (rank > 0) | (me > 0)
    has_next = (rank < n_ctx - 1) | (me < n_head - 1)
    prev_dev = (jnp.where(me > 0, rank, rank - 1), jnp.where(me > 0, me - 1, n_head - 1))
    next_dev = (
        jnp.where(me < n_head - 1, rank, rank + 1),
        jnp.where(me < n_head - 1, me + 1, 0),
    )
    outer_prev = (me == 0) & (rank > 0)
    outer_next = (me == n_head - 1) & (rank < n_ctx - 1)
    lends = (rank > 0) & (rank < n_ctx - 2)

    barrier = pltpu.get_barrier_semaphore()
    for d in range(1, n_head):
        pl.semaphore_signal(barrier, inc=1, device_id=(rank, peer(d)), device_id_type=MESH)

    def greet(k, c):
        pl.semaphore_signal(
            barrier, inc=1, device_id=(lax.rem(rank + k, n_ctx), me), device_id_type=MESH
        )
        return c

    lax.fori_loop(1, n_ctx, greet, 0)

    @pl.when(outer_prev)
    def _():
        pl.semaphore_signal(barrier, inc=1, device_id=prev_dev, device_id_type=MESH)

    @pl.when(outer_next)
    def _():
        pl.semaphore_signal(barrier, inc=1, device_id=next_dev, device_id_type=MESH)

    for u, (source, raw) in enumerate(((q_hbm, q_raw), (g_hbm, g_raw))):
        for k in range(n_head):
            for j in range(per):
                pltpu.make_async_copy(
                    source.at[pl.ds(j * BLOCK, BLOCK), pl.ds(k * heads, heads)],
                    raw.at[k, j],
                    load_sem.at[u],
                ).start()

    def wanted_by(s, c):
        best = jnp.int32(0)
        for i in range(blocks):
            at = s * blocks + i
            for j in range(NEAR, n_slot):
                local = pair_tab[j, at] - first
                named = (kind_tab[j, at] > 0) & (local >= 0) & (local < blocks)
                best = jnp.where(named, jnp.maximum(best, local), best)
        want[s] = best
        return c

    @pl.when(lends)
    def _():
        lax.fori_loop(rank + 2, n_ctx, wanted_by, 0)

    for i in range(blocks):
        for f in range(n_far):
            at = first + i
            owner[i * n_far + f] = jnp.where(
                kind_tab[NEAR + f, at] > 0, lax.div(pair_tab[NEAR + f, at], blocks), rank
            )

    @pl.when(jnp.logical_not(has_prev))
    def _():
        kv_prev[...] = jnp.zeros_like(kv_prev)

    for at, source in ((0, k_ref), (width, v_ref)):
        wide[...] = source[...].astype(f32)
        for h in range(n_head):
            head_rows = wide[pl.ds(h, rows, stride=n_head), :]
            kv_own[h, :, :, at : at + width] = head_rows.reshape(per, BLOCK, width).astype(bf16)

    extra = outer_prev.astype(jnp.int32) + outer_next.astype(jnp.int32)
    pl.semaphore_wait(barrier, n_ctx + n_head - 2 + extra)

    def kv_copy(p):
        return remote(
            kv_own.at[p],
            kv_loc.at[pl.ds(me * per, per)],
            kv_sem.at[0],
            kv_sem.at[1],
            (rank, p),
        )

    def first_copy(p):
        return remote(kv_own.at[p, 0], kv_loc.at[0], kv_sem.at[0], kv_sem.at[1], (rank, p))

    def stat_copy(u, p):
        return remote(
            (log_ref, delta_ref)[u].at[:, pl.ds(pl.multiple_of(p * rows, rows), rows)],
            stat_land.at[u, me],
            stat_sem.at[0],
            stat_sem.at[1],
            (rank, p),
        )

    def prev_copy():
        return remote(
            kv_own.at[:, per - 1], kv_prev, prev_sem.at[0], prev_sem.at[1], next_dev
        )

    @pl.when((rank == 0) & (me == 0))
    def _():
        for d in far_first:
            first_copy(peer(d)).start()
        kv_loc[0] = kv_own[0, 0]

    for u in range(2):
        for d in far_first:
            stat_copy(u, peer(d)).start()

    @pl.when(lends)
    def _():
        for d in far_first:
            kv_copy(peer(d)).start()
        kv_loc[pl.ds(me * per, per)] = kv_own[me]

    @pl.when(jnp.logical_not(lends) & has_next)
    def _():
        prev_copy().start()

    for u, source in enumerate((log_ref, delta_ref)):
        stat_land[u, me] = source[:, pl.ds(pl.multiple_of(me * rows, rows), rows)]

    arrive(q_raw, load_sem.at[0])
    arrive(g_raw, load_sem.at[1])

    def flatten(t, c):
        k, j = t // per, lax.rem(t, per)
        for raw, flat in ((q_raw, q_flat), (g_raw, g_flat)):
            flat[k, j] = raw[k, j].astype(f32).reshape(lanes, width).astype(bf16)
        return c

    lax.fori_loop(0, n_head * per, flatten, 0)

    def arr_copy(s):
        return remote(
            outgoing.at[s], arrived.at[rank], arr_send.at[s], arr_recv.at[rank], (s, me)
        )

    @pl.when(rank == 0)
    def _():
        @pl.when(me > 0)
        def _():
            arrive(kv_loc.at[0], kv_sem.at[1])

        def send_first(i, c):
            s = n_ctx - 1 - i
            outgoing[s] = kv_loc[0]
            arr_copy(s).start()
            return c

        lax.fori_loop(0, n_ctx - 1, send_first, 0)
        arrived[0] = kv_loc[0]

    arrive(stat_land.at[:, pl.ds(0, others)], stat_sem.at[1])
    spread = (
        lax.broadcasted_iota(jnp.int32, (BLOCK, lanes), 1) // heads
        == lax.broadcasted_iota(jnp.int32, (BLOCK, lanes), 0)
    ).astype(bf16)
    own_row = lax.broadcasted_iota(jnp.int32, (heads, lanes), 1) % heads == lax.broadcasted_iota(
        jnp.int32, (heads, lanes), 0
    )
    stats = stat_land[...].reshape(2 * n_head * heads, rows)
    high = stats.astype(bf16)
    rest = stats - high.astype(f32)
    mid = rest.astype(bf16)
    low = (rest - mid.astype(f32)).astype(bf16)
    for j in range(per):
        at = slice(j * BLOCK, (j + 1) * BLOCK)
        by_lane = sum(
            jnp.dot(part_of[:, at], spread, preferred_element_type=f32)
            for part_of in (high, mid, low)
        ).reshape(2 * n_head, heads, lanes)
        stat_rows[j] = jnp.sum(jnp.where(own_row[None], by_lane, 0.0), axis=1)

    key_row = lax.broadcasted_iota(jnp.int32, (2 * BLOCK, lanes), 0)
    causal = (key_row >= BLOCK) | (
        key_row <= lax.broadcasted_iota(jnp.int32, (2 * BLOCK, lanes), 1) // heads
    )
    pair_row = lax.broadcasted_iota(jnp.int32, (2 * BLOCK, 1), 0)

    def grads(k, j, kv, live):
        return tile_grads(
            kv[:, :width],
            kv[:, width:],
            q_flat[k, j],
            g_flat[k, j],
            stat_rows[j, pl.ds(k, 1)],
            stat_rows[j, pl.ds(n_head + k, 1)],
            live,
            scale,
        )

    def dq_copy(k, j):
        return pltpu.make_async_copy(
            dq_buf.at[k, j],
            dq_out.at[
                pl.ds(j * BLOCK, BLOCK), pl.ds(pl.multiple_of(k * heads, heads), heads)
            ],
            dq_sem.at[0],
        )

    def finish(k, j, total):
        dq_buf[k, j] = (total * scale).reshape(BLOCK, heads, width).astype(bf16)
        dq_copy(k, j).start()

    own_acc[...] = jnp.zeros_like(own_acc)

    def near(j):
        prev_kind = kind_tab[1, first + me * per + j]
        near_live = causal & (jnp.where(pair_row < BLOCK, 1, prev_kind) > 0)

        def near_step(k, c):
            before = kv_prev[k] if j == 0 else kv_own[k, j - 1]
            kv = jnp.concatenate([kv_own[k, j], before], axis=0)
            dq, dk, dv = grads(k, j, kv, near_live)
            if j == 0:
                finish(k, j, dq_acc[k, j] + dq)
            else:
                dq_acc[k, j] = dq
            for u, terms in enumerate((dk, dv)):
                own_acc[u, k, j] += terms[:BLOCK]
                if j == 0:
                    prev_part[k, u] = terms[BLOCK:]
                else:
                    own_acc[u, k, j - 1] += terms[BLOCK:]
            return c

        lax.fori_loop(0, n_head, near_step, 0, unroll=2)

    def send_block(i, c):
        s = n_ctx - 1 - i
        outgoing[s] = kv_loc[want[s]]
        arr_copy(s).start()
        return c

    @pl.when(lends)
    def _():
        arrive(kv_loc.at[pl.ds(0, others * per)], kv_sem.at[1])
        lax.fori_loop(0, n_ctx - 2 - rank, send_block, 0)
        arrived[rank] = kv_loc[0]

        @pl.when(has_next)
        def _():
            prev_copy().start()

    @pl.when(rank >= n_ctx - 2)
    def _():
        arrived[rank] = kv_own[0, 0]

    for j in range(1, per):
        near(j)

    def arr_wait(o, c):
        arrive(arrived.at[o], arr_recv.at[o])
        return c

    @pl.when(rank > 0)
    def _():
        arr_wait(0, 0)

    def hub_copy(p):
        return remote(arrived.at[0], hub_kv.at[me], hub_sem.at[0], hub_sem.at[1], (rank, p))

    for d in far_first:
        hub_copy(peer(d)).start()
    hub_kv[me] = arrived[0]

    lax.fori_loop(1, rank - 1, arr_wait, 0)

    def far_copy(p):
        return remote(far_send.at[p], far_kv.at[me], far_sem.at[0], far_sem.at[1], (rank, p))

    def fill_far(buf, at, p):
        for i in range(here_far):
            buf[at, i] = arrived[owner[p * here_far + i]]

    for d in far_first:
        p = peer(d)
        fill_far(far_send, p, p)
        far_copy(p).start()
    fill_far(far_kv, me, me)

    arrive(hub_kv.at[pl.ds(0, others)], hub_sem.at[1])

    pairs = n_head // 2
    tens = [2 * i for i in range(1, pairs)]

    def hred_copy(d):
        slot = 0 if d == 1 else d // 2
        return remote(
            hub_part.at[peer(d)], hub_land.at[slot], hred_sem.at[0], hred_sem.at[1], (rank, peer(d))
        )

    def pair_copy(d):
        return remote(
            hub_part.at[peer(d + 1)],
            hub_pair.at[d // 2],
            pair_sem.at[0],
            pair_sem.at[1],
            (rank, peer(1)),
        )

    def hub_step(k):
        for j in range(per):
            kind = kind_tab[NEAR - 1, first + me * per + j]
            dq, dk, dv = grads(k, j, hub_kv[k], kind > 0)
            dq_acc[k, j] = dq if j == 0 else dq_acc[k, j] + dq
            for u, terms in enumerate((dk, dv)):
                if j == 0:
                    hub_part[k, u] = terms
                else:
                    hub_part[k, u] += terms

    for d in tens:
        hub_step(peer(d + 1))
        pair_copy(d).start()
    for d in tens + [1]:
        hub_step(peer(d))
    hred_copy(1).start()
    arrive(hub_pair.at[pl.ds(1, pairs - 1)], pair_sem.at[1])
    for d in tens:
        hub_part[peer(d)] += hub_pair[d // 2]
        hred_copy(d).start()
    hub_step(me)

    arrive(far_kv.at[pl.ds(0, others)], far_sem.at[1])

    def red_copy(c, k):
        return remote(
            far_part.at[k, c], far_land.at[me, c], red_send.at[0], red_recv.at[c], (rank, k)
        )

    def far_step(k):
        for j in range(per):
            total = dq_acc[k, j]
            for f in range(n_far):
                i = j * n_far + f
                kind = kind_tab[NEAR + f, first + me * per + j]
                dq, dk, dv = grads(k, j, far_kv[k, i], kind > 0)
                total += dq
                for u, terms in enumerate((dk, dv)):
                    for b in range(cuts):
                        far_part[k, u * cuts + b, i] = terms[b * piece : (b + 1) * piece]
            if j == 0:
                dq_acc[k, j] = total
            else:
                finish(k, j, total)

    for d in across:
        far_step(peer(d))
        red_copy(0, peer(d)).start()
    for c in range(1, chunks):
        for d in across:
            red_copy(c, peer(d)).start()
    far_step(peer(1))
    for c in range(chunks):
        red_copy(c, peer(1)).start()
    far_step(me)

    @pl.when(has_prev)
    def _():
        arrive(kv_prev, prev_sem.at[1])

    near(0)

    def back_copy():
        return remote(prev_part, prev_land, back_sem.at[0], back_sem.at[1], prev_dev)

    arrive(hub_land, hred_sem.at[1])
    hub_sum[...] = sum((hub_land[i] for i in range(pairs)), hub_part[me])

    def tree_copy(i):
        return remote(
            hub_sum, hub_tree.at[i], tree_send.at[0], tree_recv.at[i], (rank - 2**i, me)
        )

    def tree_up(i):
        @pl.when(lax.rem(rank, 2 ** (i + 1)) == 2**i)
        def _():
            tree_copy(i).start()

    def tree_take(i):
        @pl.when((lax.rem(rank, 2 ** (i + 1)) == 0) & (rank + 2**i < n_ctx))
        def _():
            arrive(hub_tree.at[i], tree_recv.at[i])
            hub_sum[...] += hub_tree[i]

    tree_up(0)

    def ret_copy(c, o):
        return remote(part.at[o, c], ret.at[c, rank], ret_send.at[o], ret_recv.at[c, rank], (o, me))

    sources = [(peer(d), far_land) for d in range(1, n_head)] + [(me, far_part)]
    for c in range(chunks):
        arrive(far_land.at[pl.ds(0, others), c], red_recv.at[c])

        def send_part(o, carry):
            terms = jnp.zeros((piece, width), f32)
            for p, buf in sources:
                for i in range(here_far):
                    mine = owner[p * here_far + i] == o
                    terms += jnp.where(mine, buf[p, c, i], 0.0)
            part[o, c] = terms
            ret_copy(c, o).start()
            return carry

        lax.fori_loop(1, rank - 1, send_part, 0)
        if c == cuts - 1:
            tree_take(0)
            if stages > 1:
                tree_up(1)

    @pl.when(has_prev)
    def _():
        back_copy().start()

    for i in range(1, stages):
        tree_take(i)
        if i + 1 < stages:
            tree_up(i + 1)

    def last_copy():
        return remote(hub_sum, hub_last.at[me], last_sem.at[0], last_sem.at[1], (rank, 0))

    @pl.when((rank == 0) & (me > 0))
    def _():
        last_copy().start()

    def blk_copy(c, p):
        return remote(
            blk_part.at[p, c], blk_land.at[me, c], blk_send.at[0], blk_recv.at[c], (rank, p)
        )

    @pl.when(lends)
    def _():
        blk_part[...] = jnp.zeros_like(blk_part)
        for c in range(chunks):

            def take_part(s, carry):
                arrive(ret.at[c, s], ret_recv.at[c, s])
                for i in range(blocks):
                    blk_part[i // per, c, i % per] += jnp.where(want[s] == i, ret[c, s], 0.0)
                return carry

            lax.fori_loop(rank + 2, n_ctx, take_part, 0)
            for d in far_first:
                blk_copy(c, peer(d)).start()

    @pl.when(has_next)
    def _():
        arrive(prev_land, back_sem.at[1])
        for k in range(n_head):
            for u in range(2):
                own_acc[u, k, per - 1] += prev_land[k, u]

    @pl.when((rank == 0) & (me == 0))
    def _():
        for u in range(2):
            own_acc[u, 0, 0] += hub_sum[u]
        arrive(hub_last.at[pl.ds(0, others)], last_sem.at[1])
        for k in range(1, n_head):
            for u in range(2):
                own_acc[u, k, 0] += hub_last[k, u]

    @pl.when(lends)
    def _():
        for c in range(chunks):
            u, at = c // cuts, pl.ds(c % cuts * piece, piece)
            own_acc[u, me, :, at] += blk_part[me, c]
            arrive(blk_land.at[pl.ds(0, others), c], blk_recv.at[c])
            for d in range(1, n_head):
                own_acc[u, peer(d), :, at] += blk_land[peer(d), c]

    for u, out in ((0, dk_out), (1, dv_out)):
        for h in range(n_head):
            terms = own_acc[u, h].reshape(rows, width)
            wide[pl.ds(h, rows, stride=n_head), :] = terms * scale if u == 0 else terms
        out[...] = wide[...].astype(bf16)

    def sent_block(s, c):
        arr_copy(s).wait_send()
        return c

    lax.fori_loop(jnp.where(rank == 0, 1, rank + 2), n_ctx, sent_block, 0)

    def sent_part(o, c):
        arrive(part.at[o], ret_send.at[o])
        return c

    lax.fori_loop(1, rank - 1, sent_part, 0)
    arrive(stat_land.at[:, pl.ds(0, others)], stat_sem.at[0])
    arrive(hub_kv.at[pl.ds(0, others)], hub_sem.at[0])
    arrive(far_kv.at[pl.ds(0, others)], far_sem.at[0])
    arrive(hub_land, hred_sem.at[0])
    arrive(hub_pair.at[pl.ds(1, pairs - 1)], pair_sem.at[0])
    arrive(far_land.at[pl.ds(0, others)], red_send.at[0])

    @pl.when((rank == 0) & (me == 0))
    def _():
        arrive(kv_loc.at[pl.ds(0, others)], kv_sem.at[0])

    @pl.when(lends)
    def _():
        arrive(kv_loc.at[pl.ds(0, others * per)], kv_sem.at[0])
        arrive(blk_land.at[pl.ds(0, others)], blk_send.at[0])

    @pl.when(rank > 0)
    def _():
        arrive(hub_sum, tree_send.at[0])

    @pl.when((rank == 0) & (me > 0))
    def _():
        arrive(hub_sum, last_sem.at[0])

    @pl.when(has_next)
    def _():
        prev_copy().wait_send()

    @pl.when(has_prev)
    def _():
        back_copy().wait_send()

    arrive(dq_buf, dq_sem.at[0])


def tail(dq_in, dk_in, dv_in, dq_out, dk_out, dv_out, dq_held, dk_held, dv_held, loads, stores):
    pieces = loads.shape[0] - 2
    step = dq_held.shape[0] // pieces
    parts = [pl.ds(k * step, step) for k in range(pieces)]
    routes = [(dq_in.at[at], dq_held.at[at], dq_out.at[at]) for at in parts]
    routes += [(dk_in, dk_held, dk_out), (dv_in, dv_held, dv_out)]
    for k, (source, held, _) in enumerate(routes):
        pltpu.make_async_copy(source, held, loads.at[k]).start()
    for k, (source, held, target) in enumerate(routes):
        pltpu.make_async_copy(source, held, loads.at[k]).wait()
        pltpu.make_async_copy(held, target, stores.at[k]).start()
    for k, (_, held, target) in enumerate(routes):
        pltpu.make_async_copy(held, target, stores.at[k]).wait()


def shards(
    n_ctx,
    n_head,
    queries,
    key_states,
    value_states,
    out_grad,
    log_sums,
    row_deltas,
    block_pairs,
    pair_kinds,
):
    rows, all_heads, width = queries.shape
    heads = all_heads // n_head
    n_slot = block_pairs.shape[1]
    n_far = n_slot - NEAR
    per = rows // BLOCK
    blocks = per * n_head
    lanes = BLOCK * heads
    n_far_here = per * n_far
    stages = (n_ctx - 1).bit_length()
    bf16, f32 = jnp.bfloat16, jnp.float32
    flat = (rows * n_head, width)
    kv = (BLOCK, 2 * width)
    term = (BLOCK, width)
    piece = (BLOCK // CUTS, width)
    chunks = 2 * CUTS
    vmem = pl.BlockSpec(memory_space=pltpu.VMEM)
    smem = pl.BlockSpec(memory_space=pltpu.SMEM)
    anywhere = pl.BlockSpec(memory_space=pl.ANY)
    dma = pltpu.SemaphoreType.DMA
    raw = pltpu.VMEM((n_head, per, BLOCK, heads, width), bf16)
    rolled = pltpu.VMEM((n_head, per, lanes, width), bf16)
    dq, dk, dv = pl.pallas_call(
        partial(kernel, n_ctx, n_head, n_slot),
        out_shape=(
            jax.ShapeDtypeStruct(queries.shape, bf16),
            jax.ShapeDtypeStruct(flat, bf16),
            jax.ShapeDtypeStruct(flat, bf16),
        ),
        in_specs=[smem, smem, anywhere, anywhere, vmem, vmem, vmem, vmem],
        out_specs=(anywhere, vmem, vmem),
        scratch_shapes=[
            pltpu.VMEM(flat, f32),
            pltpu.VMEM((n_head, per) + kv, bf16),
            pltpu.VMEM((blocks,) + kv, bf16),
            pltpu.VMEM((n_head,) + kv, bf16),
            pltpu.VMEM((n_ctx,) + kv, bf16),
            pltpu.VMEM((n_ctx,) + kv, bf16),
            pltpu.VMEM((n_head, n_far_here) + kv, bf16),
            pltpu.VMEM((n_head, n_far_here) + kv, bf16),
            pltpu.VMEM((n_head,) + kv, bf16),
            raw,
            raw,
            rolled,
            rolled,
            pltpu.VMEM((2, n_head, heads, rows), f32),
            pltpu.VMEM((per, 2 * n_head, lanes), f32),
            pltpu.VMEM((n_head, per, lanes, width), f32),
            raw,
            pltpu.VMEM((2, n_head, per) + term, f32),
            pltpu.VMEM((n_head, 2) + term, f32),
            pltpu.VMEM((n_head, 2) + term, f32),
            pltpu.VMEM((n_head, chunks, n_far_here) + piece, f32),
            pltpu.VMEM((n_head, chunks, n_far_here) + piece, f32),
            pltpu.VMEM((n_head, 2) + term, f32),
            pltpu.VMEM((n_head // 2, 2) + term, f32),
            pltpu.VMEM((n_head // 2, 2) + term, f32),
            pltpu.VMEM((2,) + term, f32),
            pltpu.VMEM((stages, 2) + term, f32),
            pltpu.VMEM((n_head, 2) + term, f32),
            pltpu.VMEM((n_ctx, chunks) + piece, f32),
            pltpu.VMEM((chunks, n_ctx) + piece, f32),
            pltpu.VMEM((n_head, chunks, per) + piece, f32),
            pltpu.VMEM((n_head, chunks, per) + piece, f32),
            pltpu.SMEM((n_ctx,), jnp.int32),
            pltpu.SMEM((blocks * n_far,), jnp.int32),
            dma((2,)),
            dma((2,)),
            dma((2,)),
            dma((2,)),
            dma((n_ctx,)),
            dma((n_ctx,)),
            dma((2,)),
            dma((2,)),
            dma((1,)),
            dma((2,)),
            dma((2,)),
            dma((2,)),
            dma((1,)),
            dma((stages,)),
            dma((2,)),
            dma((1,)),
            dma((chunks,)),
            dma((n_ctx,)),
            dma((chunks, n_ctx)),
            dma((1,)),
            dma((chunks,)),
        ],
        compiler_params=pltpu.CompilerParams(
            collective_id=0, has_side_effects=True, vmem_limit_bytes=60 * 1024 * 1024
        ),
    )(
        block_pairs.T,
        pair_kinds.T,
        queries,
        out_grad,
        key_states.reshape(flat),
        value_states.reshape(flat),
        log_sums,
        row_deltas,
    )
    dq, dk, dv = pl.pallas_call(
        tail,
        out_shape=(
            jax.ShapeDtypeStruct(queries.shape, bf16),
            jax.ShapeDtypeStruct(flat, bf16),
            jax.ShapeDtypeStruct(flat, bf16),
        ),
        in_specs=[anywhere] * 3,
        out_specs=(anywhere,) * 3,
        scratch_shapes=[
            pltpu.VMEM(queries.shape, bf16),
            pltpu.VMEM(flat, bf16),
            pltpu.VMEM(flat, bf16),
            dma((6,)),
            dma((6,)),
        ],
    )(dq, dk, dv)
    return dq, dk.reshape(key_states.shape), dv.reshape(value_states.shape)


def solution(mesh):
    tokens = P(("ctx", "head"), None, None)
    stats = P("head", "ctx")
    return jax.shard_map(
        partial(shards, mesh.shape["ctx"], mesh.shape["head"]),
        mesh=mesh,
        in_specs=(tokens, tokens, tokens, tokens, stats, stats, P(), P()),
        out_specs=(tokens, tokens, tokens),
        check_vma=False,
    )
```

time: 53.8 us -> 46.3 us (0.86)
  the two profiles are of different devices: /device:TPU:11 before, /device:TPU:0 now
where the time goes in v2:
time: 46.3 us; the launch traced here: 46.1 us
  Pallas kernels  45.5 us (98%)
  between operations  0.64 us (1%)
    pallas_call x1, Pallas kernels, shards(): pl.pallas_call(partial(kernel, n_ctx, n_head, n_slot), out_shape=(jax.Sha...  43.4 us
    pallas_call x1, Pallas kernels, shards(): pl.pallas_call(tail, out_shape=(jax.ShapeDtypeStruct(queries.shape, bf16)...  2.1 us

profile of v2, /device:TPU:0, one launch (start us, length us, event | category | flops | bytes accessed | tf_op | source)
XLA Modules:
  0.0 46.1 jit_solution(3385394192152348856)
XLA Ops:
  0.6 43.4 %shard_map.103 = (bf16[128,32,128]{2,1,0:T(8,128)(2,1)}, bf16[512,128]{1,0:T(8,128)(2,1)}, bf16[512,128]{1,0:T(8,128)(2,1)}) custom-call(s32[4,64]{1,0:T(4,128)} %bitcast.8, s32[4,64]{1,0:T(4,128)} %bitcast.9, bf16[128,32,128]{2,1,0:T(8,128)(2,1)} %q_hbm.1, bf16[128,32,128]{2,1,0:T(8,128)(2,1)} %g_hbm.1, bf16[512,128]{1,0:T(8,128)(2,1)} %bitcast.6, ...), custom_call_target="tpu_custom_call" | custom-call | tf_op jit(solution)/shard_map/pallas_call | solution.py:713
  44.0 2.1 %shard_map.104 = (bf16[128,32,128]{2,1,0:T(8,128)(2,1)}, bf16[512,128]{1,0:T(8,128)(2,1)}, bf16[512,128]{1,0:T(8,128)(2,1)}) custom-call(bf16[128,32,128]{2,1,0:T(8,128)(2,1)} %get-tuple-element.9.dq_in, bf16[512,128]{1,0:T(8,128)(2,1)} %get-tuple-element.10.dk_in, bf16[512,128]{1,0:T(8,128)(2,1)} %get-tuple-element.11.dv_in), custom_call_target="tpu_custom_call" | custom-call | tf_op jit(solution)/shard_map/pallas_call | solution.py:792

commit v3 on v2

--- a/solution.py
+++ b/solution.py
@@ -43,10 +43,12 @@
     dv_out,
     wide,
     kv_own,
-    kv_loc,
+    k_loc,
+    v_loc,
     kv_prev,
     outgoing,
-    arrived,
+    k_arrived,
+    v_arrived,
     far_send,
     far_kv,
     hub_kv,
@@ -96,7 +98,9 @@
     ret_recv,
     blk_send,
     blk_recv,
+    ready,
 ):
+    kv_loc, arrived = (k_loc, v_loc), (k_arrived, v_arrived)
     rank = lax.axis_index("ctx")
     me = lax.axis_index("head")
     rows = q_hbm.shape[0]
@@ -107,7 +111,6 @@
     lanes = BLOCK * heads
     n_far = n_slot - NEAR
     here_far = per * n_far
-    stages = tree_recv.shape[0]
     chunks, piece = part.shape[1], part.shape[2]
     cuts = BLOCK // piece
     others = n_head - 1
@@ -150,17 +153,11 @@
     for d in range(1, n_head):
         pl.semaphore_signal(barrier, inc=1, device_id=(rank, peer(d)), device_id_type=MESH)
 
-    def greet(k, c):
-        pl.semaphore_signal(
-            barrier, inc=1, device_id=(lax.rem(rank + k, n_ctx), me), device_id_type=MESH
-        )
+    def greet(s, c):
+        pl.semaphore_signal(barrier, inc=1, device_id=(s, me), device_id_type=MESH)
         return c
 
-    lax.fori_loop(1, n_ctx, greet, 0)
-
-    @pl.when(outer_prev)
-    def _():
-        pl.semaphore_signal(barrier, inc=1, device_id=prev_dev, device_id_type=MESH)
+    lax.fori_loop(rank + 1, n_ctx, greet, 0)
 
     @pl.when(outer_next)
     def _():
@@ -201,26 +198,42 @@
     def _():
         kv_prev[...] = jnp.zeros_like(kv_prev)
 
-    for at, source in ((0, k_ref), (width, v_ref)):
+    for at, source in enumerate((k_ref, v_ref)):
         wide[...] = source[...].astype(f32)
         for h in range(n_head):
             head_rows = wide[pl.ds(h, rows, stride=n_head), :]
-            kv_own[h, :, :, at : at + width] = head_rows.reshape(per, BLOCK, width).astype(bf16)
-
-    extra = outer_prev.astype(jnp.int32) + outer_next.astype(jnp.int32)
-    pl.semaphore_wait(barrier, n_ctx + n_head - 2 + extra)
-
-    def kv_copy(p):
-        return remote(
-            kv_own.at[p],
-            kv_loc.at[pl.ds(me * per, per)],
+            kv_own[at, h] = head_rows.reshape(per, BLOCK, width).astype(bf16)
+
+    pl.semaphore_wait(barrier, others + rank + outer_prev.astype(jnp.int32))
+
+    def answer(o, c):
+        pl.semaphore_signal(ready, inc=1, device_id=(o, me), device_id_type=MESH)
+        return c
+
+    lax.fori_loop(0, rank, answer, 0)
+
+    @pl.when(outer_prev)
+    def _():
+        pl.semaphore_signal(ready, inc=1, device_id=prev_dev, device_id_type=MESH)
+
+    def await_ready():
+        @pl.when(rank < n_ctx - 1)
+        def _():
+            pl.semaphore_wait(ready, n_ctx - 1 - rank + outer_next.astype(jnp.int32))
+
+    def kv_copy(a, p):
+        return remote(
+            kv_own.at[a, p],
+            kv_loc[a].at[pl.ds(me * per, per)],
             kv_sem.at[0],
-            kv_sem.at[1],
+            kv_sem.at[1 + a],
             (rank, p),
         )
 
-    def first_copy(p):
-        return remote(kv_own.at[p, 0], kv_loc.at[0], kv_sem.at[0], kv_sem.at[1], (rank, p))
+    def first_copy(a, p):
+        return remote(
+            kv_own.at[a, p, 0], kv_loc[a].at[0], kv_sem.at[0], kv_sem.at[1 + a], (rank, p)
+        )
 
     def stat_copy(u, p):
         return remote(
@@ -233,14 +246,15 @@
 
     def prev_copy():
         return remote(
-            kv_own.at[:, per - 1], kv_prev, prev_sem.at[0], prev_sem.at[1], next_dev
+            kv_own.at[:, :, per - 1], kv_prev, prev_sem.at[0], prev_sem.at[1], next_dev
         )
 
     @pl.when((rank == 0) & (me == 0))
     def _():
-        for d in far_first:
-            first_copy(peer(d)).start()
-        kv_loc[0] = kv_own[0, 0]
+        for a in range(2):
+            for d in far_first:
+                first_copy(a, peer(d)).start()
+            kv_loc[a][0] = kv_own[a, 0, 0]
 
     for u in range(2):
         for d in far_first:
@@ -248,47 +262,40 @@
 
     @pl.when(lends)
     def _():
-        for d in far_first:
-            kv_copy(peer(d)).start()
-        kv_loc[pl.ds(me * per, per)] = kv_own[me]
-
-    @pl.when(jnp.logical_not(lends) & has_next)
-    def _():
-        prev_copy().start()
+        for a in range(2):
+            for d in far_first:
+                kv_copy(a, peer(d)).start()
+        for a in range(2):
+            kv_loc[a][pl.ds(me * per, per)] = kv_own[a, me]
 
     for u, source in enumerate((log_ref, delta_ref)):
         stat_land[u, me] = source[:, pl.ds(pl.multiple_of(me * rows, rows), rows)]
 
-    arrive(q_raw, load_sem.at[0])
-    arrive(g_raw, load_sem.at[1])
-
-    def flatten(t, c):
-        k, j = t // per, lax.rem(t, per)
-        for raw, flat in ((q_raw, q_flat), (g_raw, g_flat)):
-            flat[k, j] = raw[k, j].astype(f32).reshape(lanes, width).astype(bf16)
-        return c
-
-    lax.fori_loop(0, n_head * per, flatten, 0)
-
-    def arr_copy(s):
-        return remote(
-            outgoing.at[s], arrived.at[rank], arr_send.at[s], arr_recv.at[rank], (s, me)
+    def arr_copy(a, s):
+        return remote(
+            outgoing.at[a, s], arrived[a].at[rank], arr_send.at[s], arr_recv.at[a, rank], (s, me)
         )
 
     @pl.when(rank == 0)
     def _():
         @pl.when(me > 0)
         def _():
-            arrive(kv_loc.at[0], kv_sem.at[1])
+            for a in range(2):
+                arrive(kv_loc[a].at[0], kv_sem.at[1 + a])
+
+        await_ready()
 
         def send_first(i, c):
             s = n_ctx - 1 - i
-            outgoing[s] = kv_loc[0]
-            arr_copy(s).start()
+            for a in range(2):
+                outgoing[a, s] = kv_loc[a][0]
+                arr_copy(a, s).start()
             return c
 
         lax.fori_loop(0, n_ctx - 1, send_first, 0)
-        arrived[0] = kv_loc[0]
+        for a in range(2):
+            arrived[a][0] = kv_loc[a][0]
+        prev_copy().start()
 
     arrive(stat_land.at[:, pl.ds(0, others)], stat_sem.at[1])
     spread = (
@@ -317,10 +324,10 @@
     )
     pair_row = lax.broadcasted_iota(jnp.int32, (2 * BLOCK, 1), 0)
 
-    def grads(k, j, kv, live):
+    def grads(k, j, keys, values, live):
         return tile_grads(
-            kv[:, :width],
-            kv[:, width:],
+            keys,
+            values,
             q_flat[k, j],
             g_flat[k, j],
             stat_rows[j, pl.ds(k, 1)],
@@ -342,18 +349,36 @@
         dq_buf[k, j] = (total * scale).reshape(BLOCK, heads, width).astype(bf16)
         dq_copy(k, j).start()
 
+    arrive(q_raw, load_sem.at[0])
+    arrive(g_raw, load_sem.at[1])
+
+    def flatten(t, c):
+        k, j = t // per, lax.rem(t, per)
+        for raw, flat in ((q_raw, q_flat), (g_raw, g_flat)):
+            flat[k, j] = raw[k, j].astype(f32).reshape(lanes, width).astype(bf16)
+        return c
+
+    lax.fori_loop(0, n_head * per, flatten, 0)
+
     own_acc[...] = jnp.zeros_like(own_acc)
-
-    def near(j):
+    dq_acc[:, 0] = jnp.zeros((n_head, lanes, width), f32)
+
+    def near(j, lo, hi):
         prev_kind = kind_tab[1, first + me * per + j]
         near_live = causal & (jnp.where(pair_row < BLOCK, 1, prev_kind) > 0)
 
         def near_step(k, c):
-            before = kv_prev[k] if j == 0 else kv_own[k, j - 1]
-            kv = jnp.concatenate([kv_own[k, j], before], axis=0)
-            dq, dk, dv = grads(k, j, kv, near_live)
+            keys, values = (
+                jnp.concatenate(
+                    [kv_own[a, k, j], kv_prev[a, k] if j == 0 else kv_own[a, k, j - 1]], axis=0
+                )
+                for a in range(2)
+            )
+            dq, dk, dv = grads(k, j, keys, values, near_live)
             if j == 0:
-                finish(k, j, dq_acc[k, j] + dq)
+                finish(k, 0, dq_acc[k, 0] + dq)
+                for other in range(1, per):
+                    finish(k, other, dq_acc[k, other])
             else:
                 dq_acc[k, j] = dq
             for u, terms in enumerate((dk, dv)):
@@ -364,105 +389,84 @@
                     own_acc[u, k, j - 1] += terms[BLOCK:]
             return c
 
-        lax.fori_loop(0, n_head, near_step, 0, unroll=2)
-
-    def send_block(i, c):
-        s = n_ctx - 1 - i
-        outgoing[s] = kv_loc[want[s]]
-        arr_copy(s).start()
-        return c
-
-    @pl.when(lends)
-    def _():
-        arrive(kv_loc.at[pl.ds(0, others * per)], kv_sem.at[1])
-        lax.fori_loop(0, n_ctx - 2 - rank, send_block, 0)
-        arrived[rank] = kv_loc[0]
+        lax.fori_loop(lo, hi, near_step, 0, unroll=2)
+
+    half = n_head // 2
+
+    def send_block(a):
+        def send(i, c):
+            s = n_ctx - 1 - i
+            outgoing[a, s] = kv_loc[a][want[s]]
+            arr_copy(a, s).start()
+            return c
+
+        lax.fori_loop(0, n_ctx - 2 - rank, send, 0)
+
+    def lend(a):
+        @pl.when(lends)
+        def _():
+            arrive(kv_loc[a].at[pl.ds(0, others * per)], kv_sem.at[1 + a])
+            if a == 0:
+                await_ready()
+            send_block(a)
+            arrived[a][rank] = kv_loc[a][0]
+            if a == 1:
+                prev_copy().start()
+
+    lend(0)
+
+    @pl.when(rank >= n_ctx - 2)
+    def _():
+        await_ready()
+        for a in range(2):
+            arrived[a][rank] = kv_own[a, 0, 0]
 
         @pl.when(has_next)
         def _():
             prev_copy().start()
 
-    @pl.when(rank >= n_ctx - 2)
-    def _():
-        arrived[rank] = kv_own[0, 0]
-
     for j in range(1, per):
-        near(j)
-
-    def arr_wait(o, c):
-        arrive(arrived.at[o], arr_recv.at[o])
-        return c
+        near(j, 0, half)
+    lend(1)
+    for j in range(1, per):
+        near(j, half, n_head)
 
     @pl.when(rank > 0)
     def _():
-        arr_wait(0, 0)
-
-    def hub_copy(p):
-        return remote(arrived.at[0], hub_kv.at[me], hub_sem.at[0], hub_sem.at[1], (rank, p))
-
-    for d in far_first:
-        hub_copy(peer(d)).start()
-    hub_kv[me] = arrived[0]
-
-    lax.fori_loop(1, rank - 1, arr_wait, 0)
-
-    def far_copy(p):
-        return remote(far_send.at[p], far_kv.at[me], far_sem.at[0], far_sem.at[1], (rank, p))
-
-    def fill_far(buf, at, p):
+        for a in range(2):
+            arrive(arrived[a].at[0], arr_recv.at[a, 0])
+
+    for a in range(2):
+        for d in far_first:
+            remote(
+                arrived[a].at[0], hub_kv.at[a, me], hub_sem.at[0], hub_sem.at[1], (rank, peer(d))
+            ).start()
+        hub_kv[a, me] = arrived[a][0]
+
+    def far_copy(a, d):
+        return remote(
+            far_send.at[a, peer(d)],
+            far_kv.at[a, me],
+            far_sem.at[0],
+            far_sem.at[1 if d == 1 else 2 + a],
+            (rank, peer(d)),
+        )
+
+    def fill_far(buf, a, p):
         for i in range(here_far):
-            buf[at, i] = arrived[owner[p * here_far + i]]
-
-    for d in far_first:
-        p = peer(d)
-        fill_far(far_send, p, p)
-        far_copy(p).start()
-    fill_far(far_kv, me, me)
-
-    arrive(hub_kv.at[pl.ds(0, others)], hub_sem.at[1])
-
-    pairs = n_head // 2
-    tens = [2 * i for i in range(1, pairs)]
-
-    def hred_copy(d):
-        slot = 0 if d == 1 else d // 2
-        return remote(
-            hub_part.at[peer(d)], hub_land.at[slot], hred_sem.at[0], hred_sem.at[1], (rank, peer(d))
-        )
-
-    def pair_copy(d):
-        return remote(
-            hub_part.at[peer(d + 1)],
-            hub_pair.at[d // 2],
-            pair_sem.at[0],
-            pair_sem.at[1],
-            (rank, peer(1)),
-        )
-
-    def hub_step(k):
-        for j in range(per):
-            kind = kind_tab[NEAR - 1, first + me * per + j]
-            dq, dk, dv = grads(k, j, hub_kv[k], kind > 0)
-            dq_acc[k, j] = dq if j == 0 else dq_acc[k, j] + dq
-            for u, terms in enumerate((dk, dv)):
-                if j == 0:
-                    hub_part[k, u] = terms
-                else:
-                    hub_part[k, u] += terms
-
-    for d in tens:
-        hub_step(peer(d + 1))
-        pair_copy(d).start()
-    for d in tens + [1]:
-        hub_step(peer(d))
-    hred_copy(1).start()
-    arrive(hub_pair.at[pl.ds(1, pairs - 1)], pair_sem.at[1])
-    for d in tens:
-        hub_part[peer(d)] += hub_pair[d // 2]
-        hred_copy(d).start()
-    hub_step(me)
-
-    arrive(far_kv.at[pl.ds(0, others)], far_sem.at[1])
+            buf[a, p, i] = arrived[a][owner[p * here_far + i]]
+
+    for a in range(2):
+
+        def arr_wait(o, c):
+            arrive(arrived[a].at[o], arr_recv.at[a, o])
+            return c
+
+        lax.fori_loop(1, rank - 1, arr_wait, 0)
+        for d in far_first:
+            fill_far(far_send, a, peer(d))
+            far_copy(a, d).start()
+        fill_far(far_kv, a, me)
 
     def red_copy(c, k):
         return remote(
@@ -475,15 +479,62 @@
             for f in range(n_far):
                 i = j * n_far + f
                 kind = kind_tab[NEAR + f, first + me * per + j]
-                dq, dk, dv = grads(k, j, far_kv[k, i], kind > 0)
+                dq, dk, dv = grads(k, j, far_kv[0, k, i], far_kv[1, k, i], kind > 0)
                 total += dq
                 for u, terms in enumerate((dk, dv)):
                     for b in range(cuts):
                         far_part[k, u * cuts + b, i] = terms[b * piece : (b + 1) * piece]
-            if j == 0:
-                dq_acc[k, j] = total
-            else:
-                finish(k, j, total)
+            dq_acc[k, j] = total
+
+    far_step(me)
+    arrive(far_kv.at[:, 0], far_sem.at[1])
+    far_step(peer(1))
+    for c in range(chunks):
+        red_copy(c, peer(1)).start()
+
+    arrive(hub_kv.at[:, pl.ds(0, others)], hub_sem.at[1])
+
+    pairs = n_head // 2
+    tens = [2 * i for i in range(1, pairs)]
+
+    def hred_copy(d):
+        slot = 0 if d == 1 else d // 2
+        return remote(
+            hub_part.at[peer(d)], hub_land.at[slot], hred_sem.at[0], hred_sem.at[1], (rank, peer(d))
+        )
+
+    def pair_copy(d):
+        return remote(
+            hub_part.at[peer(d + 1)],
+            hub_pair.at[d // 2],
+            pair_sem.at[0],
+            pair_sem.at[1],
+            (rank, peer(1)),
+        )
+
+    def hub_step(k):
+        for j in range(per):
+            kind = kind_tab[NEAR - 1, first + me * per + j]
+            dq, dk, dv = grads(k, j, hub_kv[0, k], hub_kv[1, k], kind > 0)
+            dq_acc[k, j] += dq
+            for u, terms in enumerate((dk, dv)):
+                if j == 0:
+                    hub_part[k, u] = terms
+                else:
+                    hub_part[k, u] += terms
+
+    for d in tens:
+        hub_step(peer(d + 1))
+        pair_copy(d).start()
+    for d in tens:
+        hub_step(peer(d))
+    arrive(hub_pair.at[pl.ds(1, pairs - 1)], pair_sem.at[1])
+    for d in tens:
+        hub_part[peer(d)] += hub_pair[d // 2]
+        hred_copy(d).start()
+
+    for a in range(2):
+        arrive(far_kv.at[a, pl.ds(0, others - 1)], far_sem.at[2 + a])
 
     for d in across:
         far_step(peer(d))
@@ -491,46 +542,33 @@
     for c in range(1, chunks):
         for d in across:
             red_copy(c, peer(d)).start()
-    far_step(peer(1))
-    for c in range(chunks):
-        red_copy(c, peer(1)).start()
-    far_step(me)
-
-    @pl.when(has_prev)
-    def _():
-        arrive(kv_prev, prev_sem.at[1])
-
-    near(0)
-
-    def back_copy():
-        return remote(prev_part, prev_land, back_sem.at[0], back_sem.at[1], prev_dev)
-
-    arrive(hub_land, hred_sem.at[1])
-    hub_sum[...] = sum((hub_land[i] for i in range(pairs)), hub_part[me])
-
-    def tree_copy(i):
-        return remote(
-            hub_sum, hub_tree.at[i], tree_send.at[0], tree_recv.at[i], (rank - 2**i, me)
-        )
-
-    def tree_up(i):
-        @pl.when(lax.rem(rank, 2 ** (i + 1)) == 2**i)
-        def _():
-            tree_copy(i).start()
-
-    def tree_take(i):
-        @pl.when((lax.rem(rank, 2 ** (i + 1)) == 0) & (rank + 2**i < n_ctx))
-        def _():
-            arrive(hub_tree.at[i], tree_recv.at[i])
-            hub_sum[...] += hub_tree[i]
-
-    tree_up(0)
+
+    hub_step(peer(1))
+    hred_copy(1).start()
+    hub_step(me)
+
+    def tree_copy():
+        odd = lax.rem(rank, 2)
+        slot = jnp.where(odd == 1, 0, rank // 2)
+        return remote(
+            hub_sum,
+            hub_tree.at[slot],
+            tree_send.at[0],
+            tree_recv.at[slot],
+            (jnp.where(odd == 1, rank - 1, 0), me),
+        )
+
+    def tree_take(i, c):
+        arrive(hub_tree.at[i], tree_recv.at[i])
+        hub_sum[...] += hub_tree[i]
+        return c
 
     def ret_copy(c, o):
         return remote(part.at[o, c], ret.at[c, rank], ret_send.at[o], ret_recv.at[c, rank], (o, me))
 
     sources = [(peer(d), far_land) for d in range(1, n_head)] + [(me, far_part)]
-    for c in range(chunks):
+
+    def reduce(c):
         arrive(far_land.at[pl.ds(0, others), c], red_recv.at[c])
 
         def send_part(o, carry):
@@ -544,19 +582,45 @@
             return carry
 
         lax.fori_loop(1, rank - 1, send_part, 0)
-        if c == cuts - 1:
-            tree_take(0)
-            if stages > 1:
-                tree_up(1)
+
+    def back_copy():
+        return remote(prev_part, prev_land, back_sem.at[0], back_sem.at[1], prev_dev)
 
     @pl.when(has_prev)
     def _():
+        arrive(kv_prev, prev_sem.at[1])
+
+    reduce(0)
+    arrive(hub_land, hred_sem.at[1])
+    hub_sum[...] = sum((hub_land[i] for i in range(pairs)), hub_part[me])
+
+    @pl.when(lax.rem(rank, 2) == 1)
+    def _():
+        tree_copy().start()
+
+    near(0, 0, half)
+    reduce(1)
+    near(0, half, n_head)
+    for c in range(2, min(3, chunks)):
+        reduce(c)
+    @pl.when((lax.rem(rank, 2) == 0) & (rank + 1 < n_ctx))
+    def _():
+        tree_take(0, 0)
+
+        @pl.when(rank > 0)
+        def _():
+            tree_copy().start()
+
+    for c in range(3, chunks):
+        reduce(c)
+
+    @pl.when(has_prev)
+    def _():
         back_copy().start()
 
-    for i in range(1, stages):
-        tree_take(i)
-        if i + 1 < stages:
-            tree_up(i + 1)
+    @pl.when(rank == 0)
+    def _():
+        lax.fori_loop(1, (n_ctx + 1) // 2, tree_take, 0)
 
     def last_copy():
         return remote(hub_sum, hub_last.at[me], last_sem.at[0], last_sem.at[1], (rank, 0))
@@ -617,7 +681,7 @@
         out[...] = wide[...].astype(bf16)
 
     def sent_block(s, c):
-        arr_copy(s).wait_send()
+        arrive(outgoing.at[:, s], arr_send.at[s])
         return c
 
     lax.fori_loop(jnp.where(rank == 0, 1, rank + 2), n_ctx, sent_block, 0)
@@ -628,19 +692,19 @@
 
     lax.fori_loop(1, rank - 1, sent_part, 0)
     arrive(stat_land.at[:, pl.ds(0, others)], stat_sem.at[0])
-    arrive(hub_kv.at[pl.ds(0, others)], hub_sem.at[0])
-    arrive(far_kv.at[pl.ds(0, others)], far_sem.at[0])
+    arrive(hub_kv.at[:, pl.ds(0, others)], hub_sem.at[0])
+    arrive(far_kv.at[:, pl.ds(0, others)], far_sem.at[0])
     arrive(hub_land, hred_sem.at[0])
     arrive(hub_pair.at[pl.ds(1, pairs - 1)], pair_sem.at[0])
     arrive(far_land.at[pl.ds(0, others)], red_send.at[0])
 
     @pl.when((rank == 0) & (me == 0))
     def _():
-        arrive(kv_loc.at[pl.ds(0, others)], kv_sem.at[0])
+        arrive(hub_kv.at[:, pl.ds(0, others)], kv_sem.at[0])
 
     @pl.when(lends)
     def _():
-        arrive(kv_loc.at[pl.ds(0, others * per)], kv_sem.at[0])
+        arrive(kv_own.at[:, pl.ds(0, others)], kv_sem.at[0])
         arrive(blk_land.at[pl.ds(0, others)], blk_send.at[0])
 
     @pl.when(rank > 0)
@@ -697,10 +761,8 @@
     blocks = per * n_head
     lanes = BLOCK * heads
     n_far_here = per * n_far
-    stages = (n_ctx - 1).bit_length()
     bf16, f32 = jnp.bfloat16, jnp.float32
     flat = (rows * n_head, width)
-    kv = (BLOCK, 2 * width)
     term = (BLOCK, width)
     piece = (BLOCK // CUTS, width)
     chunks = 2 * CUTS
@@ -721,14 +783,16 @@
         out_specs=(anywhere, vmem, vmem),
         scratch_shapes=[
             pltpu.VMEM(flat, f32),
-            pltpu.VMEM((n_head, per) + kv, bf16),
-            pltpu.VMEM((blocks,) + kv, bf16),
-            pltpu.VMEM((n_head,) + kv, bf16),
-            pltpu.VMEM((n_ctx,) + kv, bf16),
-            pltpu.VMEM((n_ctx,) + kv, bf16),
-            pltpu.VMEM((n_head, n_far_here) + kv, bf16),
-            pltpu.VMEM((n_head, n_far_here) + kv, bf16),
-            pltpu.VMEM((n_head,) + kv, bf16),
+            pltpu.VMEM((2, n_head, per) + term, bf16),
+            pltpu.VMEM((blocks,) + term, bf16),
+            pltpu.VMEM((blocks,) + term, bf16),
+            pltpu.VMEM((2, n_head) + term, bf16),
+            pltpu.VMEM((2, n_ctx) + term, bf16),
+            pltpu.VMEM((n_ctx,) + term, bf16),
+            pltpu.VMEM((n_ctx,) + term, bf16),
+            pltpu.VMEM((2, n_head, n_far_here) + term, bf16),
+            pltpu.VMEM((2, n_head, n_far_here) + term, bf16),
+            pltpu.VMEM((2, n_head) + term, bf16),
             raw,
             raw,
             rolled,
@@ -746,7 +810,7 @@
             pltpu.VMEM((n_head // 2, 2) + term, f32),
             pltpu.VMEM((n_head // 2, 2) + term, f32),
             pltpu.VMEM((2,) + term, f32),
-            pltpu.VMEM((stages, 2) + term, f32),
+            pltpu.VMEM(((n_ctx + 1) // 2, 2) + term, f32),
             pltpu.VMEM((n_head, 2) + term, f32),
             pltpu.VMEM((n_ctx, chunks) + piece, f32),
             pltpu.VMEM((chunks, n_ctx) + piece, f32),
@@ -755,19 +819,19 @@
             pltpu.SMEM((n_ctx,), jnp.int32),
             pltpu.SMEM((blocks * n_far,), jnp.int32),
             dma((2,)),
-            dma((2,)),
+            dma((3,)),
             dma((2,)),
             dma((2,)),
             dma((n_ctx,)),
-            dma((n_ctx,)),
-            dma((2,)),
+            dma((2, n_ctx)),
+            dma((4,)),
             dma((2,)),
             dma((1,)),
             dma((2,)),
             dma((2,)),
             dma((2,)),
             dma((1,)),
-            dma((stages,)),
+            dma(((n_ctx + 1) // 2,)),
             dma((2,)),
             dma((1,)),
             dma((chunks,)),
@@ -775,6 +839,7 @@
             dma((chunks, n_ctx)),
             dma((1,)),
             dma((chunks,)),
+            pltpu.SemaphoreType.REGULAR,
         ],
         compiler_params=pltpu.CompilerParams(
             collective_id=0, has_side_effects=True, vmem_limit_bytes=60 * 1024 * 1024

time: 46.3 us -> 44.7 us (0.965)
  Pallas kernels: 45.5 us -> 43.8 us
    pallas_call x1, Pallas kernels: 43.4 us -> 41.7 us  [shards(): pl.pallas_call(partial(kernel, n_ctx, n_head, n_slot), out_shape=(jax.Sha...]
where the time goes in v3:
time: 44.7 us; the launch traced here: 44.5 us
  Pallas kernels  43.8 us (98%)
  between operations  0.64 us (1%)
    pallas_call x1, Pallas kernels, shards(): pl.pallas_call(partial(kernel, n_ctx, n_head, n_slot), out_shape=(jax.Sha...  41.7 us
    pallas_call x1, Pallas kernels, shards(): pl.pallas_call(tail, out_shape=(jax.ShapeDtypeStruct(queries.shape, bf16)...  2.1 us

profile of v3, /device:TPU:0, one launch (start us, length us, event | category | flops | bytes accessed | tf_op | source)
XLA Modules:
  0.0 44.5 jit_solution(17486818717425381736)
XLA Ops:
  0.6 41.7 %shard_map.103 = (bf16[128,32,128]{2,1,0:T(8,128)(2,1)}, bf16[512,128]{1,0:T(8,128)(2,1)}, bf16[512,128]{1,0:T(8,128)(2,1)}) custom-call(s32[4,64]{1,0:T(4,128)} %bitcast.8, s32[4,64]{1,0:T(4,128)} %bitcast.9, bf16[128,32,128]{2,1,0:T(8,128)(2,1)} %q_hbm.1, bf16[128,32,128]{2,1,0:T(8,128)(2,1)} %g_hbm.1, bf16[512,128]{1,0:T(8,128)(2,1)} %bitcast.6, ...), custom_call_target="tpu_custom_call" | custom-call | tf_op jit(solution)/shard_map/pallas_call | solution.py:775
  42.4 2.1 %shard_map.104 = (bf16[128,32,128]{2,1,0:T(8,128)(2,1)}, bf16[512,128]{1,0:T(8,128)(2,1)}, bf16[512,128]{1,0:T(8,128)(2,1)}) custom-call(bf16[128,32,128]{2,1,0:T(8,128)(2,1)} %get-tuple-element.9.dq_in, bf16[512,128]{1,0:T(8,128)(2,1)} %get-tuple-element.10.dk_in, bf16[512,128]{1,0:T(8,128)(2,1)} %get-tuple-element.11.dv_in), custom_call_target="tpu_custom_call" | custom-call | tf_op jit(solution)/shard_map/pallas_call | solution.py:857

commit v4 on v3

--- a/solution.py
+++ b/solution.py
@@ -38,7 +38,7 @@
     v_ref,
     log_ref,
     delta_ref,
-    dq_out,
+    dq_buf,
     dk_out,
     dv_out,
     wide,
@@ -59,7 +59,6 @@
     stat_land,
     stat_rows,
     dq_acc,
-    dq_buf,
     own_acc,
     prev_part,
     prev_land,
@@ -85,7 +84,6 @@
     arr_recv,
     far_sem,
     hub_sem,
-    dq_sem,
     back_sem,
     hred_sem,
     pair_sem,
@@ -148,6 +146,7 @@
     outer_prev = (me == 0) & (rank > 0)
     outer_next = (me == n_head - 1) & (rank < n_ctx - 1)
     lends = (rank > 0) & (rank < n_ctx - 2)
+    has_far = rank > 2
 
     barrier = pltpu.get_barrier_semaphore()
     for d in range(1, n_head):
@@ -336,18 +335,14 @@
             scale,
         )
 
-    def dq_copy(k, j):
-        return pltpu.make_async_copy(
-            dq_buf.at[k, j],
-            dq_out.at[
-                pl.ds(j * BLOCK, BLOCK), pl.ds(pl.multiple_of(k * heads, heads), heads)
-            ],
-            dq_sem.at[0],
-        )
-
-    def finish(k, j, total):
-        dq_buf[k, j] = (total * scale).reshape(BLOCK, heads, width).astype(bf16)
-        dq_copy(k, j).start()
+    def finish(lo, hi):
+        def each(k, c):
+            for j in range(per):
+                total = dq_acc[k, j] * scale
+                dq_buf[k, j] = total.reshape(BLOCK, heads, width).astype(bf16)
+            return c
+
+        lax.fori_loop(lo, hi, each, 0)
 
     arrive(q_raw, load_sem.at[0])
     arrive(g_raw, load_sem.at[1])
@@ -375,12 +370,7 @@
                 for a in range(2)
             )
             dq, dk, dv = grads(k, j, keys, values, near_live)
-            if j == 0:
-                finish(k, 0, dq_acc[k, 0] + dq)
-                for other in range(1, per):
-                    finish(k, other, dq_acc[k, other])
-            else:
-                dq_acc[k, j] = dq
+            dq_acc[k, j] = dq if j else dq_acc[k, j] + dq
             for u, terms in enumerate((dk, dv)):
                 own_acc[u, k, j] += terms[:BLOCK]
                 if j == 0:
@@ -443,6 +433,30 @@
             ).start()
         hub_kv[a, me] = arrived[a][0]
 
+    def back_copy():
+        return remote(prev_part, prev_land, back_sem.at[0], back_sem.at[1], prev_dev)
+
+    late0 = outer_prev & (lax.rem(rank, 2) == 0)
+    early_back = (
+        has_prev & jnp.logical_not(late0) & jnp.logical_not(has_far)
+    )
+    yields = late0 & lends & has_far
+
+    def near_first():
+        @pl.when(has_prev)
+        def _():
+            arrive(kv_prev, prev_sem.at[1])
+
+        near(0, 0, n_head)
+
+    @pl.when(jnp.logical_not(late0))
+    def _():
+        near_first()
+
+    @pl.when(early_back)
+    def _():
+        back_copy().start()
+
     def far_copy(a, d):
         return remote(
             far_send.at[a, peer(d)],
@@ -456,17 +470,19 @@
         for i in range(here_far):
             buf[a, p, i] = arrived[a][owner[p * here_far + i]]
 
-    for a in range(2):
-
-        def arr_wait(o, c):
-            arrive(arrived[a].at[o], arr_recv.at[a, o])
-            return c
-
-        lax.fori_loop(1, rank - 1, arr_wait, 0)
-        for d in far_first:
-            fill_far(far_send, a, peer(d))
-            far_copy(a, d).start()
-        fill_far(far_kv, a, me)
+    @pl.when(has_far)
+    def _():
+        for a in range(2):
+
+            def arr_wait(o, c):
+                arrive(arrived[a].at[o], arr_recv.at[a, o])
+                return c
+
+            lax.fori_loop(1, rank - 1, arr_wait, 0)
+            for d in far_first:
+                fill_far(far_send, a, peer(d))
+                far_copy(a, d).start()
+            fill_far(far_kv, a, me)
 
     def red_copy(c, k):
         return remote(
@@ -486,11 +502,9 @@
                         far_part[k, u * cuts + b, i] = terms[b * piece : (b + 1) * piece]
             dq_acc[k, j] = total
 
-    far_step(me)
-    arrive(far_kv.at[:, 0], far_sem.at[1])
-    far_step(peer(1))
-    for c in range(chunks):
-        red_copy(c, peer(1)).start()
+    @pl.when(has_far)
+    def _():
+        far_step(me)
 
     arrive(hub_kv.at[:, pl.ds(0, others)], hub_sem.at[1])
 
@@ -533,35 +547,48 @@
         hub_part[peer(d)] += hub_pair[d // 2]
         hred_copy(d).start()
 
-    for a in range(2):
-        arrive(far_kv.at[a, pl.ds(0, others - 1)], far_sem.at[2 + a])
-
-    for d in across:
-        far_step(peer(d))
-        red_copy(0, peer(d)).start()
-    for c in range(1, chunks):
-        for d in across:
-            red_copy(c, peer(d)).start()
-
     hub_step(peer(1))
     hred_copy(1).start()
     hub_step(me)
 
-    def tree_copy():
-        odd = lax.rem(rank, 2)
-        slot = jnp.where(odd == 1, 0, rank // 2)
-        return remote(
-            hub_sum,
-            hub_tree.at[slot],
-            tree_send.at[0],
-            tree_recv.at[slot],
-            (jnp.where(odd == 1, rank - 1, 0), me),
-        )
-
-    def tree_take(i, c):
-        arrive(hub_tree.at[i], tree_recv.at[i])
-        hub_sum[...] += hub_tree[i]
-        return c
+    @pl.when(has_far)
+    def _():
+        for a in range(2):
+            arrive(far_kv.at[a, pl.ds(0, others - 1)], far_sem.at[2 + a])
+
+        for d in across:
+            far_step(peer(d))
+            red_copy(0, peer(d)).start()
+        for c in range(1, chunks):
+            for d in across:
+                red_copy(c, peer(d)).start()
+        arrive(far_kv.at[:, 0], far_sem.at[1])
+        far_step(peer(1))
+        for c in range(chunks):
+            red_copy(c, peer(1)).start()
+
+
+    stages = tree_recv.shape[0]
+
+    def tree_copy(i):
+        return remote(
+            hub_sum, hub_tree.at[i], tree_send.at[0], tree_recv.at[i], (rank - 2**i, me)
+        )
+
+    def tree_up(i):
+        if i < stages:
+
+            @pl.when(lax.rem(rank, 2 ** (i + 1)) == 2**i)
+            def _():
+                tree_copy(i).start()
+
+    def tree_take(i):
+        if i < stages:
+
+            @pl.when((lax.rem(rank, 2 ** (i + 1)) == 0) & (rank + 2**i < n_ctx))
+            def _():
+                arrive(hub_tree.at[i], tree_recv.at[i])
+                hub_sum[...] += hub_tree[i]
 
     def ret_copy(c, o):
         return remote(part.at[o, c], ret.at[c, rank], ret_send.at[o], ret_recv.at[c, rank], (o, me))
@@ -569,6 +596,11 @@
     sources = [(peer(d), far_land) for d in range(1, n_head)] + [(me, far_part)]
 
     def reduce(c):
+        @pl.when(has_far)
+        def _():
+            reduce_live(c)
+
+    def reduce_live(c):
         arrive(far_land.at[pl.ds(0, others), c], red_recv.at[c])
 
         def send_part(o, carry):
@@ -583,44 +615,29 @@
 
         lax.fori_loop(1, rank - 1, send_part, 0)
 
-    def back_copy():
-        return remote(prev_part, prev_land, back_sem.at[0], back_sem.at[1], prev_dev)
-
-    @pl.when(has_prev)
-    def _():
-        arrive(kv_prev, prev_sem.at[1])
-
-    reduce(0)
     arrive(hub_land, hred_sem.at[1])
     hub_sum[...] = sum((hub_land[i] for i in range(pairs)), hub_part[me])
-
-    @pl.when(lax.rem(rank, 2) == 1)
-    def _():
-        tree_copy().start()
-
-    near(0, 0, half)
+    tree_up(0)
+    reduce(0)
+    @pl.when(late0)
+    def _():
+        near_first()
+
+    finish(0, half)
     reduce(1)
-    near(0, half, n_head)
-    for c in range(2, min(3, chunks)):
+    tree_take(0)
+    tree_up(1)
+    finish(half, n_head)
+    for c in range(2, chunks):
         reduce(c)
-    @pl.when((lax.rem(rank, 2) == 0) & (rank + 1 < n_ctx))
-    def _():
-        tree_take(0, 0)
-
-        @pl.when(rank > 0)
-        def _():
-            tree_copy().start()
-
-    for c in range(3, chunks):
-        reduce(c)
-
-    @pl.when(has_prev)
+
+    @pl.when(has_prev & jnp.logical_not(yields | early_back))
     def _():
         back_copy().start()
 
-    @pl.when(rank == 0)
-    def _():
-        lax.fori_loop(1, (n_ctx + 1) // 2, tree_take, 0)
+    for i in range(1, stages):
+        tree_take(i)
+        tree_up(i + 1)
 
     def last_copy():
         return remote(hub_sum, hub_last.at[me], last_sem.at[0], last_sem.at[1], (rank, 0))
@@ -648,6 +665,10 @@
             lax.fori_loop(rank + 2, n_ctx, take_part, 0)
             for d in far_first:
                 blk_copy(c, peer(d)).start()
+
+    @pl.when(yields)
+    def _():
+        back_copy().start()
 
     @pl.when(has_next)
     def _():
@@ -693,10 +714,13 @@
     lax.fori_loop(1, rank - 1, sent_part, 0)
     arrive(stat_land.at[:, pl.ds(0, others)], stat_sem.at[0])
     arrive(hub_kv.at[:, pl.ds(0, others)], hub_sem.at[0])
-    arrive(far_kv.at[:, pl.ds(0, others)], far_sem.at[0])
     arrive(hub_land, hred_sem.at[0])
     arrive(hub_pair.at[pl.ds(1, pairs - 1)], pair_sem.at[0])
-    arrive(far_land.at[pl.ds(0, others)], red_send.at[0])
+
+    @pl.when(has_far)
+    def _():
+        arrive(far_kv.at[:, pl.ds(0, others)], far_sem.at[0])
+        arrive(far_land.at[pl.ds(0, others)], red_send.at[0])
 
     @pl.when((rank == 0) & (me == 0))
     def _():
@@ -723,22 +747,23 @@
     def _():
         back_copy().wait_send()
 
-    arrive(dq_buf, dq_sem.at[0])
-
-
-def tail(dq_in, dk_in, dv_in, dq_out, dk_out, dv_out, dq_held, dk_held, dv_held, loads, stores):
-    pieces = loads.shape[0] - 2
-    step = dq_held.shape[0] // pieces
-    parts = [pl.ds(k * step, step) for k in range(pieces)]
-    routes = [(dq_in.at[at], dq_held.at[at], dq_out.at[at]) for at in parts]
-    routes += [(dk_in, dk_held, dk_out), (dv_in, dv_held, dv_out)]
-    for k, (source, held, _) in enumerate(routes):
-        pltpu.make_async_copy(source, held, loads.at[k]).start()
-    for k, (source, held, target) in enumerate(routes):
-        pltpu.make_async_copy(source, held, loads.at[k]).wait()
-        pltpu.make_async_copy(held, target, stores.at[k]).start()
-    for k, (_, held, target) in enumerate(routes):
-        pltpu.make_async_copy(held, target, stores.at[k]).wait()
+
+def tail(dq_in, dk_in, dv_in, dq_out, dk_out, dv_out, stores):
+    n_head, per, block, heads, _ = dq_in.shape
+    routes = [
+        (dq_in.at[k, j], dq_out.at[pl.ds(j * block, block), pl.ds(k * heads, heads)])
+        for k in range(n_head)
+        for j in range(per)
+    ]
+    routes += [(dk_in, dk_out), (dv_in, dv_out)]
+    copies = [
+        pltpu.make_async_copy(source, target, stores.at[i])
+        for i, (source, target) in enumerate(routes)
+    ]
+    for copy in copies:
+        copy.start()
+    for copy in copies:
+        copy.wait()
 
 
 def shards(
@@ -761,6 +786,7 @@
     blocks = per * n_head
     lanes = BLOCK * heads
     n_far_here = per * n_far
+    stages = (n_ctx - 1).bit_length()
     bf16, f32 = jnp.bfloat16, jnp.float32
     flat = (rows * n_head, width)
     term = (BLOCK, width)
@@ -774,13 +800,9 @@
     rolled = pltpu.VMEM((n_head, per, lanes, width), bf16)
     dq, dk, dv = pl.pallas_call(
         partial(kernel, n_ctx, n_head, n_slot),
-        out_shape=(
-            jax.ShapeDtypeStruct(queries.shape, bf16),
-            jax.ShapeDtypeStruct(flat, bf16),
-            jax.ShapeDtypeStruct(flat, bf16),
-        ),
+        out_shape=(raw, pltpu.VMEM(flat, bf16), pltpu.VMEM(flat, bf16)),
         in_specs=[smem, smem, anywhere, anywhere, vmem, vmem, vmem, vmem],
-        out_specs=(anywhere, vmem, vmem),
+        out_specs=(vmem, vmem, vmem),
         scratch_shapes=[
             pltpu.VMEM(flat, f32),
             pltpu.VMEM((2, n_head, per) + term, bf16),
@@ -800,7 +822,6 @@
             pltpu.VMEM((2, n_head, heads, rows), f32),
             pltpu.VMEM((per, 2 * n_head, lanes), f32),
             pltpu.VMEM((n_head, per, lanes, width), f32),
-            raw,
             pltpu.VMEM((2, n_head, per) + term, f32),
             pltpu.VMEM((n_head, 2) + term, f32),
             pltpu.VMEM((n_head, 2) + term, f32),
@@ -810,7 +831,7 @@
             pltpu.VMEM((n_head // 2, 2) + term, f32),
             pltpu.VMEM((n_head // 2, 2) + term, f32),
             pltpu.VMEM((2,) + term, f32),
-            pltpu.VMEM(((n_ctx + 1) // 2, 2) + term, f32),
+            pltpu.VMEM((stages, 2) + term, f32),
             pltpu.VMEM((n_head, 2) + term, f32),
             pltpu.VMEM((n_ctx, chunks) + piece, f32),
             pltpu.VMEM((chunks, n_ctx) + piece, f32),
@@ -826,12 +847,11 @@
             dma((2, n_ctx)),
             dma((4,)),
             dma((2,)),
-            dma((1,)),
             dma((2,)),
             dma((2,)),
             dma((2,)),
             dma((1,)),
-            dma(((n_ctx + 1) // 2,)),
+            dma((stages,)),
             dma((2,)),
             dma((1,)),
             dma((chunks,)),
@@ -861,16 +881,10 @@
             jax.ShapeDtypeStruct(flat, bf16),
             jax.ShapeDtypeStruct(flat, bf16),
         ),
-        in_specs=[anywhere] * 3,
+        in_specs=[vmem] * 3,
         out_specs=(anywhere,) * 3,
-        scratch_shapes=[
-            pltpu.VMEM(queries.shape, bf16),
-            pltpu.VMEM(flat, bf16),
-            pltpu.VMEM(flat, bf16),
-            dma((6,)),
-            dma((6,)),
-        ],
-    )(dq, dk, dv)
+        scratch_shapes=[dma((n_head * per + 2,))],
+    )(*(pltpu.with_memory_space_constraint(x, pltpu.VMEM) for x in (dq, dk, dv)))
     return dq, dk.reshape(key_states.shape), dv.reshape(value_states.shape)
 
 

time: 44.7 us -> 42.6 us (0.953); the launches traced: 44.5 us -> 41.9 us
  Pallas kernels: 43.8 us -> 41.2 us
    pallas_call x1, Pallas kernels: 41.7 us -> 40.1 us  [shards(): pl.pallas_call(partial(kernel, n_ctx, n_head, n_slot), out_shape=(raw, pl...]
    pallas_call x1, Pallas kernels: 2.1 us -> 1.13 us  [shards(): pl.pallas_call(tail, out_shape=(jax.ShapeDtypeStruct(queries.shape, bf16)...]
where the time goes in v4:
time: 42.6 us; the launch traced here: 41.9 us
  Pallas kernels  41.2 us (97%)
  between operations  0.64 us (2%)
    pallas_call x1, Pallas kernels, shards(): pl.pallas_call(partial(kernel, n_ctx, n_head, n_slot), out_shape=(raw, pl...  40.1 us
    pallas_call x1, Pallas kernels, shards(): pl.pallas_call(tail, out_shape=(jax.ShapeDtypeStruct(queries.shape, bf16)...  1.13 us

profile of v4, /device:TPU:0, one launch (start us, length us, event | category | flops | bytes accessed | tf_op | source)
XLA Modules:
  0.0 41.9 jit_solution(8852013827204886999)
XLA Ops:
  0.6 40.1 %shard_map.103 = (bf16[4,2,64,8,128]{4,3,2,1,0:T(8,128)(2,1)S(1)}, bf16[512,128]{1,0:T(8,128)(2,1)S(1)}, bf16[512,128]{1,0:T(8,128)(2,1)S(1)}) custom-call(s32[4,64]{1,0:T(4,128)} %bitcast.8, s32[4,64]{1,0:T(4,128)} %bitcast.9, bf16[128,32,128]{2,1,0:T(8,128)(2,1)} %q_hbm.1, bf16[128,32,128]{2,1,0:T(8,128)(2,1)} %g_hbm.1, bf16[512,128]{1,0:T(8,128)(2,1)} %bitcast.6, ...), custom_call_target="tpu_custom_call" | custom-call | tf_op jit(solution)/shard_map/pallas_call | solution.py:801
  40.8 1.1 %shard_map.104 = (bf16[128,32,128]{2,1,0:T(8,128)(2,1)}, bf16[512,128]{1,0:T(8,128)(2,1)}, bf16[512,128]{1,0:T(8,128)(2,1)}) custom-call(bf16[4,2,64,8,128]{4,3,2,1,0:T(8,128)(2,1)S(1)} %get-tuple-element.9.dq_in, bf16[512,128]{1,0:T(8,128)(2,1)S(1)} %get-tuple-element.10.dk_in, bf16[512,128]{1,0:T(8,128)(2,1)S(1)} %get-tuple-element.11.dv_in), custom_call_target="tpu_custom_call" | custom-call | tf_op jit(solution)/shard_map/pallas_call | solution.py:877

commit v5 on v4

--- a/solution.py
+++ b/solution.py
@@ -296,6 +296,38 @@
             arrived[a][0] = kv_loc[a][0]
         prev_copy().start()
 
+    def send_block(a):
+        def send(i, c):
+            s = n_ctx - 1 - i
+            outgoing[a, s] = kv_loc[a][want[s]]
+            arr_copy(a, s).start()
+            return c
+
+        lax.fori_loop(0, n_ctx - 2 - rank, send, 0)
+
+    def lend(a):
+        @pl.when(lends)
+        def _():
+            arrive(kv_loc[a].at[pl.ds(0, others * per)], kv_sem.at[1 + a])
+            if a == 0:
+                await_ready()
+            send_block(a)
+            arrived[a][rank] = kv_loc[a][0]
+            if a == 1:
+                prev_copy().start()
+
+    lend(0)
+
+    @pl.when(rank >= n_ctx - 2)
+    def _():
+        await_ready()
+        for a in range(2):
+            arrived[a][rank] = kv_own[a, 0, 0]
+
+        @pl.when(has_next)
+        def _():
+            prev_copy().start()
+
     arrive(stat_land.at[:, pl.ds(0, others)], stat_sem.at[1])
     spread = (
         lax.broadcasted_iota(jnp.int32, (BLOCK, lanes), 1) // heads
@@ -383,43 +415,9 @@
 
     half = n_head // 2
 
-    def send_block(a):
-        def send(i, c):
-            s = n_ctx - 1 - i
-            outgoing[a, s] = kv_loc[a][want[s]]
-            arr_copy(a, s).start()
-            return c
-
-        lax.fori_loop(0, n_ctx - 2 - rank, send, 0)
-
-    def lend(a):
-        @pl.when(lends)
-        def _():
-            arrive(kv_loc[a].at[pl.ds(0, others * per)], kv_sem.at[1 + a])
-            if a == 0:
-                await_ready()
-            send_block(a)
-            arrived[a][rank] = kv_loc[a][0]
-            if a == 1:
-                prev_copy().start()
-
-    lend(0)
-
-    @pl.when(rank >= n_ctx - 2)
-    def _():
-        await_ready()
-        for a in range(2):
-            arrived[a][rank] = kv_own[a, 0, 0]
-
-        @pl.when(has_next)
-        def _():
-            prev_copy().start()
-
-    for j in range(1, per):
-        near(j, 0, half)
     lend(1)
     for j in range(1, per):
-        near(j, half, n_head)
+        near(j, 0, n_head)
 
     @pl.when(rank > 0)
     def _():
@@ -436,11 +434,10 @@
     def back_copy():
         return remote(prev_part, prev_land, back_sem.at[0], back_sem.at[1], prev_dev)
 
-    late0 = outer_prev & (lax.rem(rank, 2) == 0)
+    late0 = outer_prev & has_far & (lax.rem(rank, 2) == 0)
     early_back = (
         has_prev & jnp.logical_not(late0) & jnp.logical_not(has_far)
     )
-    yields = late0 & lends & has_far
 
     def near_first():
         @pl.when(has_prev)
@@ -549,7 +546,6 @@
 
     hub_step(peer(1))
     hred_copy(1).start()
-    hub_step(me)
 
     @pl.when(has_far)
     def _():
@@ -615,29 +611,42 @@
 
         lax.fori_loop(1, rank - 1, send_part, 0)
 
+    @pl.when(late0)
+    def _():
+        near_first()
+
+    hub_step(me)
     arrive(hub_land, hred_sem.at[1])
     hub_sum[...] = sum((hub_land[i] for i in range(pairs)), hub_part[me])
     tree_up(0)
     reduce(0)
-    @pl.when(late0)
-    def _():
-        near_first()
+    @pl.when(jnp.logical_not(lends))
+    def _():
+        tree_take(0)
+        tree_up(1)
 
     finish(0, half)
     reduce(1)
-    tree_take(0)
-    tree_up(1)
     finish(half, n_head)
     for c in range(2, chunks):
         reduce(c)
 
-    @pl.when(has_prev & jnp.logical_not(yields | early_back))
+    @pl.when(has_prev & jnp.logical_not((late0 & lends) | early_back))
     def _():
         back_copy().start()
+
+    @pl.when(lends)
+    def _():
+        tree_take(0)
+        tree_up(1)
 
     for i in range(1, stages):
         tree_take(i)
         tree_up(i + 1)
+
+    @pl.when(late0 & lends)
+    def _():
+        back_copy().start()
 
     def last_copy():
         return remote(hub_sum, hub_last.at[me], last_sem.at[0], last_sem.at[1], (rank, 0))
@@ -665,10 +674,6 @@
             lax.fori_loop(rank + 2, n_ctx, take_part, 0)
             for d in far_first:
                 blk_copy(c, peer(d)).start()
-
-    @pl.when(yields)
-    def _():
-        back_copy().start()
 
     @pl.when(has_next)
     def _():

time: 42.6 us -> 42 us (0.986); the launches traced: 41.9 us -> 41.8 us
  no operation moved by 1% of the time
where the time goes in v5:
time: 42 us; the launch traced here: 41.8 us
  Pallas kernels  41.1 us (98%)
  between operations  0.64 us (2%)
    pallas_call x1, Pallas kernels, shards(): pl.pallas_call(partial(kernel, n_ctx, n_head, n_slot), out_shape=(raw, pl...  40 us
    pallas_call x1, Pallas kernels, shards(): pl.pallas_call(tail, out_shape=(jax.ShapeDtypeStruct(queries.shape, bf16)...  1.13 us

profile of v5, /device:TPU:0, one launch (start us, length us, event | category | flops | bytes accessed | tf_op | source)
XLA Modules:
  0.0 41.8 jit_solution(6356662969082202351)
XLA Ops:
  0.6 40.0 %shard_map.103 = (bf16[4,2,64,8,128]{4,3,2,1,0:T(8,128)(2,1)S(1)}, bf16[512,128]{1,0:T(8,128)(2,1)S(1)}, bf16[512,128]{1,0:T(8,128)(2,1)S(1)}) custom-call(s32[4,64]{1,0:T(4,128)} %bitcast.8, s32[4,64]{1,0:T(4,128)} %bitcast.9, bf16[128,32,128]{2,1,0:T(8,128)(2,1)} %q_hbm.1, bf16[128,32,128]{2,1,0:T(8,128)(2,1)} %g_hbm.1, bf16[512,128]{1,0:T(8,128)(2,1)} %bitcast.6, ...), custom_call_target="tpu_custom_call" | custom-call | tf_op jit(solution)/shard_map/pallas_call | solution.py:806
  40.7 1.1 %shard_map.104 = (bf16[128,32,128]{2,1,0:T(8,128)(2,1)}, bf16[512,128]{1,0:T(8,128)(2,1)}, bf16[512,128]{1,0:T(8,128)(2,1)}) custom-call(bf16[4,2,64,8,128]{4,3,2,1,0:T(8,128)(2,1)S(1)} %get-tuple-element.9.dq_in, bf16[512,128]{1,0:T(8,128)(2,1)S(1)} %get-tuple-element.10.dk_in, bf16[512,128]{1,0:T(8,128)(2,1)S(1)} %get-tuple-element.11.dv_in), custom_call_target="tpu_custom_call" | custom-call | tf_op jit(solution)/shard_map/pallas_call | solution.py:882

commit v6 on v5

--- a/solution.py
+++ b/solution.py
@@ -547,6 +547,11 @@
     hub_step(peer(1))
     hred_copy(1).start()
 
+    @pl.when(late0 & lends)
+    def _():
+        near_first()
+        back_copy().start()
+
     @pl.when(has_far)
     def _():
         for a in range(2):
@@ -566,28 +571,45 @@
 
     stages = tree_recv.shape[0]
 
-    def tree_copy(i):
-        return remote(
-            hub_sum, hub_tree.at[i], tree_send.at[0], tree_recv.at[i], (rank - 2**i, me)
-        )
-
-    def tree_up(i):
+    def tree_copy(i, u):
+        return remote(
+            hub_sum.at[u],
+            hub_tree.at[i, u],
+            tree_send.at[0],
+            tree_recv.at[i, u],
+            (rank - 2**i, me),
+        )
+
+    def tree_up(i, u):
         if i < stages:
 
             @pl.when(lax.rem(rank, 2 ** (i + 1)) == 2**i)
             def _():
-                tree_copy(i).start()
-
-    def tree_take(i):
-        if i < stages:
-
-            @pl.when((lax.rem(rank, 2 ** (i + 1)) == 0) & (rank + 2**i < n_ctx))
-            def _():
-                arrive(hub_tree.at[i], tree_recv.at[i])
-                hub_sum[...] += hub_tree[i]
+                tree_copy(i, u).start()
+
+    def tree_step(i):
+        for u in range(2):
+            if i < stages:
+
+                @pl.when((lax.rem(rank, 2 ** (i + 1)) == 0) & (rank + 2**i < n_ctx))
+                def _():
+                    arrive(hub_tree.at[i, u], tree_recv.at[i, u])
+                    hub_sum[u] += hub_tree[i, u]
+
+            tree_up(i + 1, u)
+            if i == stages - 1:
+
+                @pl.when((rank == 0) & (me > 0))
+                def _():
+                    last_copy(u).start()
+
+    def last_copy(u):
+        return remote(
+            hub_sum.at[u], hub_last.at[me, u], last_sem.at[0], last_sem.at[1 + u], (rank, 0)
+        )
 
     def ret_copy(c, o):
-        return remote(part.at[o, c], ret.at[c, rank], ret_send.at[o], ret_recv.at[c, rank], (o, me))
+        return remote(part.at[o, c], ret.at[c, rank], ret_send.at[o - 1], ret_recv.at[c, rank - NEAR], (o, me))
 
     sources = [(peer(d), far_land) for d in range(1, n_head)] + [(me, far_part)]
 
@@ -611,19 +633,19 @@
 
         lax.fori_loop(1, rank - 1, send_part, 0)
 
-    @pl.when(late0)
+    @pl.when(late0 & jnp.logical_not(lends))
     def _():
         near_first()
 
     hub_step(me)
     arrive(hub_land, hred_sem.at[1])
     hub_sum[...] = sum((hub_land[i] for i in range(pairs)), hub_part[me])
-    tree_up(0)
+    for u in range(2):
+        tree_up(0, u)
     reduce(0)
     @pl.when(jnp.logical_not(lends))
     def _():
-        tree_take(0)
-        tree_up(1)
+        tree_step(0)
 
     finish(0, half)
     reduce(1)
@@ -637,23 +659,10 @@
 
     @pl.when(lends)
     def _():
-        tree_take(0)
-        tree_up(1)
+        tree_step(0)
 
     for i in range(1, stages):
-        tree_take(i)
-        tree_up(i + 1)
-
-    @pl.when(late0 & lends)
-    def _():
-        back_copy().start()
-
-    def last_copy():
-        return remote(hub_sum, hub_last.at[me], last_sem.at[0], last_sem.at[1], (rank, 0))
-
-    @pl.when((rank == 0) & (me > 0))
-    def _():
-        last_copy().start()
+        tree_step(i)
 
     def blk_copy(c, p):
         return remote(
@@ -666,7 +675,7 @@
         for c in range(chunks):
 
             def take_part(s, carry):
-                arrive(ret.at[c, s], ret_recv.at[c, s])
+                arrive(ret.at[c, s], ret_recv.at[c, s - NEAR])
                 for i in range(blocks):
                     blk_part[i // per, c, i % per] += jnp.where(want[s] == i, ret[c, s], 0.0)
                 return carry
@@ -686,9 +695,8 @@
     def _():
         for u in range(2):
             own_acc[u, 0, 0] += hub_sum[u]
-        arrive(hub_last.at[pl.ds(0, others)], last_sem.at[1])
-        for k in range(1, n_head):
-            for u in range(2):
+            arrive(hub_last.at[pl.ds(0, others), u], last_sem.at[1 + u])
+            for k in range(1, n_head):
                 own_acc[u, k, 0] += hub_last[k, u]
 
     @pl.when(lends)
@@ -713,7 +721,7 @@
     lax.fori_loop(jnp.where(rank == 0, 1, rank + 2), n_ctx, sent_block, 0)
 
     def sent_part(o, c):
-        arrive(part.at[o], ret_send.at[o])
+        arrive(part.at[o], ret_send.at[o - 1])
         return c
 
     lax.fori_loop(1, rank - 1, sent_part, 0)
@@ -849,19 +857,19 @@
             dma((2,)),
             dma((2,)),
             dma((n_ctx,)),
-            dma((2, n_ctx)),
+            dma((2, n_ctx - 2)),
             dma((4,)),
             dma((2,)),
             dma((2,)),
             dma((2,)),
             dma((2,)),
             dma((1,)),
-            dma((stages,)),
-            dma((2,)),
+            dma((stages, 2)),
+            dma((3,)),
             dma((1,)),
             dma((chunks,)),
-            dma((n_ctx,)),
-            dma((chunks, n_ctx)),
+            dma((n_ctx - NEAR,)),
+            dma((chunks, n_ctx - NEAR)),
             dma((1,)),
             dma((chunks,)),
             pltpu.SemaphoreType.REGULAR,

time: 42 us -> 41.9 us (level)
  no operation moved by 1% of the time
where the time goes in v6:
time: 41.9 us; the launch traced here: 41.7 us
  Pallas kernels  41.1 us (98%)
  between operations  0.64 us (2%)
    pallas_call x1, Pallas kernels, shards(): pl.pallas_call(partial(kernel, n_ctx, n_head, n_slot), out_shape=(raw, pl...  40 us
    pallas_call x1, Pallas kernels, shards(): pl.pallas_call(tail, out_shape=(jax.ShapeDtypeStruct(queries.shape, bf16)...  1.13 us

profile of v6, /device:TPU:0, one launch (start us, length us, event | category | flops | bytes accessed | tf_op | source)
XLA Modules:
  0.0 41.7 jit_solution(7293818211565111170)
XLA Ops:
  0.6 40.0 %shard_map.103 = (bf16[4,2,64,8,128]{4,3,2,1,0:T(8,128)(2,1)S(1)}, bf16[512,128]{1,0:T(8,128)(2,1)S(1)}, bf16[512,128]{1,0:T(8,128)(2,1)S(1)}) custom-call(s32[4,64]{1,0:T(4,128)} %bitcast.8, s32[4,64]{1,0:T(4,128)} %bitcast.9, bf16[128,32,128]{2,1,0:T(8,128)(2,1)} %q_hbm.1, bf16[128,32,128]{2,1,0:T(8,128)(2,1)} %g_hbm.1, bf16[512,128]{1,0:T(8,128)(2,1)} %bitcast.6, ...), custom_call_target="tpu_custom_call" | custom-call | tf_op jit(solution)/shard_map/pallas_call | solution.py:814
  40.6 1.1 %shard_map.104 = (bf16[128,32,128]{2,1,0:T(8,128)(2,1)}, bf16[512,128]{1,0:T(8,128)(2,1)}, bf16[512,128]{1,0:T(8,128)(2,1)}) custom-call(bf16[4,2,64,8,128]{4,3,2,1,0:T(8,128)(2,1)S(1)} %get-tuple-element.9.dq_in, bf16[512,128]{1,0:T(8,128)(2,1)S(1)} %get-tuple-element.10.dk_in, bf16[512,128]{1,0:T(8,128)(2,1)S(1)} %get-tuple-element.11.dv_in), custom_call_target="tpu_custom_call" | custom-call | tf_op jit(solution)/shard_map/pallas_call | solution.py:890

commit v7 on v6

--- a/solution.py
+++ b/solution.py
@@ -650,18 +650,25 @@
     finish(0, half)
     reduce(1)
     finish(half, n_head)
-    for c in range(2, chunks):
+    for c in range(2, chunks - 1):
         reduce(c)
+    @pl.when(lends)
+    def _():
+        tree_step(0)
+        tree_step(1)
+
+    reduce(chunks - 1)
 
     @pl.when(has_prev & jnp.logical_not((late0 & lends) | early_back))
     def _():
         back_copy().start()
 
-    @pl.when(lends)
-    def _():
-        tree_step(0)
-
-    for i in range(1, stages):
+
+    @pl.when(jnp.logical_not(lends))
+    def _():
+        tree_step(1)
+
+    for i in range(2, stages):
         tree_step(i)
 
     def blk_copy(c, p):

time: 41.9 us -> 41.3 us (0.986)
  Pallas kernels: 41.1 us -> 40.5 us
    pallas_call x1, Pallas kernels: 40 us -> 39.4 us  [shards(): pl.pallas_call(partial(kernel, n_ctx, n_head, n_slot), out_shape=(raw, pl...]
where the time goes in v7:
time: 41.3 us; the launch traced here: 41.2 us
  Pallas kernels  40.5 us (98%)
  between operations  0.64 us (2%)
    pallas_call x1, Pallas kernels, shards(): pl.pallas_call(partial(kernel, n_ctx, n_head, n_slot), out_shape=(raw, pl...  39.4 us
    pallas_call x1, Pallas kernels, shards(): pl.pallas_call(tail, out_shape=(jax.ShapeDtypeStruct(queries.shape, bf16)...  1.13 us

profile of v7, /device:TPU:0, one launch (start us, length us, event | category | flops | bytes accessed | tf_op | source)
XLA Modules:
  0.0 41.2 jit_solution(16593286077010063634)
XLA Ops:
  0.6 39.4 %shard_map.103 = (bf16[4,2,64,8,128]{4,3,2,1,0:T(8,128)(2,1)S(1)}, bf16[512,128]{1,0:T(8,128)(2,1)S(1)}, bf16[512,128]{1,0:T(8,128)(2,1)S(1)}) custom-call(s32[4,64]{1,0:T(4,128)} %bitcast.8, s32[4,64]{1,0:T(4,128)} %bitcast.9, bf16[128,32,128]{2,1,0:T(8,128)(2,1)} %q_hbm.1, bf16[128,32,128]{2,1,0:T(8,128)(2,1)} %g_hbm.1, bf16[512,128]{1,0:T(8,128)(2,1)} %bitcast.6, ...), custom_call_target="tpu_custom_call" | custom-call | tf_op jit(solution)/shard_map/pallas_call | solution.py:821
  40.0 1.1 %shard_map.104 = (bf16[128,32,128]{2,1,0:T(8,128)(2,1)}, bf16[512,128]{1,0:T(8,128)(2,1)}, bf16[512,128]{1,0:T(8,128)(2,1)}) custom-call(bf16[4,2,64,8,128]{4,3,2,1,0:T(8,128)(2,1)S(1)} %get-tuple-element.9.dq_in, bf16[512,128]{1,0:T(8,128)(2,1)S(1)} %get-tuple-element.10.dk_in, bf16[512,128]{1,0:T(8,128)(2,1)S(1)} %get-tuple-element.11.dv_in), custom_call_target="tpu_custom_call" | custom-call | tf_op jit(solution)/shard_map/pallas_call | solution.py:897
